TPU v7x, 128 devices: a whole 4x4x4 slice. The times are simulated.
128 devices in a mesh: ka: 16 (over y, z), cfg: 8 (over x, core).
Axes of the slice: x: 4, y: 4, z: 4, core: 2. Of those that a mesh axis runs over, the one named last changes fastest.
Arguments:
- medium_t: float32 [2, 2, 16, 16, 16], replicated, may hold values from -6 to 6
- structure: float32 [2, 2, 16, 16, 16384], P(None, None, None, None, ('ka', 'cfg')), may hold values from -0.12 to 0.12
- kmap: int32 [16384], P(('ka', 'cfg')), may hold values from 0 to 15, as said below
- occupation: int32 [128, 16], P(('ka', 'cfg')), may hold values from 0 to 1
- cfg_weight: float32 [128], P(('ka', 'cfg')), may hold values from 1 to 30
- shift_a: float32 [2, 2, 16, 16], replicated, may hold values from -0.18 to 0.18
- shift_b: float32 [2, 2, 16, 16], replicated, may hold values from -0.18 to 0.18
Outputs:
- coarse_tau: float32 [2, 2, 16, 16, 16], replicated
- avg_tau: float32 [2, 2, 256, 256], P(None, None, 'cfg')
- correction: float32 [2, 2, 16384], P(None, None, ('ka', 'cfg'))
Inputs may be any that keep to these rules, and one draw needn't show every extreme that they name: `kmap`: every cluster momentum is named by exactly 16384 / 16 k-points.
All inputs are finite; a program needn't handle non-finite values.
Results may differ from a plain program's by a relative error of at most 0.00015.
Values sent between devices are 32-bit elements; how exact they have to be, the bound alone decides.
A program may use at most 128 MiB of HBM per device.

v0:
```python
import math

import jax
import jax.numpy as jnp
from jax import lax
from jax.sharding import PartitionSpec as P

ENERGIES = 2
TERMS = 3


HIGH = lax.Precision.HIGHEST


def phase_tables(count_sites):
    places = jnp.arange(count_sites, dtype=jnp.int32)
    half_n = count_sites // 2
    cell = places % half_n
    site_xyz = jnp.stack([cell // 4, cell // 2 % 2, cell % 2], axis=1).astype(jnp.float32)
    site_xyz = site_xyz + 0.5 * (places >= half_n).astype(jnp.float32)[:, None]
    mom_hkl = jnp.stack([places // 4, places // 2 % 2, places % 2], axis=1).astype(jnp.float32)
    angles = math.pi * jnp.sum(mom_hkl[:, None, :] * site_xyz[None, :, :], axis=2)
    differ = angles[:, :, None] - angles[:, None, :]
    return (jnp.cos(differ), jnp.sin(differ))


def batch_mul(first_m, second_m):

    def single(left_m, right_m):
        return jnp.einsum("abk,bck->ack", left_m, right_m, precision=HIGH)

    return jnp.stack(
        [
            single(first_m[0], second_m[0]) - single(first_m[1], second_m[1]),
            single(first_m[0], second_m[1]) + single(first_m[1], second_m[0]),
        ]
    )


def batch_trace(first_m, second_m):

    def single(left_m, right_m):
        return jnp.einsum("abk,bak->k", left_m, right_m, precision=HIGH)

    return jnp.stack(
        [
            single(first_m[0], second_m[0]) - single(first_m[1], second_m[1]),
            single(first_m[0], second_m[1]) + single(first_m[1], second_m[0]),
        ]
    )


def kpoint_terms(medium, structure, onehot):
    spread_m = jnp.einsum("xabm,mk->xabk", medium, onehot, precision=HIGH)
    factor_m = batch_mul(spread_m, structure)
    second_t = batch_mul(factor_m, spread_m)
    third_t = batch_mul(factor_m, second_t)
    kpoint_tau = spread_m + second_t + third_t
    partial_sum = jnp.einsum("xabk,mk->xabm", kpoint_tau, onehot, precision=HIGH)
    return (partial_sum, batch_mul(kpoint_tau, kpoint_tau))


def to_cluster(moment_tau, cosine, sine_tab):
    count_sites = cosine.shape[1]
    chans = moment_tau.shape[1]

    def apply_phase(table, block):
        return jnp.einsum("mij,abm->iajb", table, block, precision=HIGH)

    real_part = (
        apply_phase(cosine, moment_tau[0]) - apply_phase(sine_tab, moment_tau[1])
    ) / count_sites
    imag_part = (
        apply_phase(cosine, moment_tau[1]) + apply_phase(sine_tab, moment_tau[0])
    ) / count_sites
    order_n = count_sites * chans
    return jnp.stack([real_part.reshape(order_n, order_n), imag_part.reshape(order_n, order_n)])


def to_moment(cluster_rows, cosine_rows, sine_rows):
    count_sites = cosine_rows.shape[2]
    chans = cluster_rows.shape[2] // count_sites
    real_in = cluster_rows[0].reshape(-1, chans, count_sites, chans)
    imag_in = cluster_rows[1].reshape(-1, chans, count_sites, chans)

    def apply_phase(table, block):
        return jnp.einsum("mij,iajb->abm", table, block, precision=HIGH)

    real_part = (apply_phase(cosine_rows, real_in) + apply_phase(sine_rows, imag_in)) / count_sites
    imag_part = (apply_phase(cosine_rows, imag_in) - apply_phase(sine_rows, real_in)) / count_sites
    return jnp.stack([real_part, imag_part])


def impurity_sum(cluster, shift_first, shift_second, occupied, weights):
    count_cfg, count_sites = occupied.shape
    order_n = cluster.shape[1]
    chans = order_n // count_sites
    share = occupied.astype(jnp.float32)[None, :, :, None, None]
    delta = share * shift_first[:, None, None] + (1.0 - share) * shift_second[:, None, None]
    current = cluster[:, None]

    def site_mul(left_m, right_m):
        return jnp.einsum("gsab,gsbc->gsac", left_m, right_m, precision=HIGH)

    def left_mul(left_m, right_m):
        return jnp.einsum("ij,gjc->gic", left_m, right_m, precision=HIGH)

    for sweep_idx in range(TERMS):
        blocks = current.reshape(2, count_cfg, count_sites, chans, order_n)
        scattered = jnp.stack(
            [
                site_mul(delta[0], blocks[0]) - site_mul(delta[1], blocks[1]),
                site_mul(delta[0], blocks[1]) + site_mul(delta[1], blocks[0]),
            ]
        )
        scattered = scattered.reshape(2, count_cfg, order_n, order_n)
        product = jnp.stack(
            [
                left_mul(cluster[0], scattered[0]) - left_mul(cluster[1], scattered[1]),
                left_mul(cluster[0], scattered[1]) + left_mul(cluster[1], scattered[0]),
            ]
        )
        current = cluster[:, None] - product
    return jnp.einsum("g,xgij->xij", weights, current, precision=HIGH)


def per_device(medium_t, structure, kmap, occupation, cfg_weight, shift_a, shift_b):
    count_sites = occupation.shape[1]
    count_moms = medium_t.shape[-1]
    chans = medium_t.shape[2]
    order_n = count_sites * chans
    all_devices = lax.axis_size("ka") * lax.axis_size("cfg")
    all_kpoints = kmap.shape[0] * all_devices
    per_moment = all_kpoints // count_moms
    cosine, sine_tab = phase_tables(count_sites)
    onehot = (kmap[None, :] == jnp.arange(count_moms, dtype=jnp.int32)[:, None]).astype(jnp.float32)
    partial_list = []
    square_list = []
    for energy in range(ENERGIES):
        partial_sum, squared = kpoint_terms(medium_t[energy], structure[energy], onehot)
        partial_list.append(partial_sum)
        square_list.append(squared)
    summed, weight_total = lax.psum((jnp.stack(partial_list), jnp.sum(cfg_weight)), ("ka", "cfg"))
    coarse = summed / per_moment
    owner_rows_n = order_n // lax.axis_size("cfg")
    row_start = lax.axis_index("cfg") * owner_rows_n
    local_list = []
    for energy in range(ENERGIES):
        cluster = to_cluster(coarse[energy], cosine, sine_tab)
        local_list.append(
            impurity_sum(cluster, shift_a[energy], shift_b[energy], occupation, cfg_weight)
        )
    scaled = jnp.stack(local_list) / weight_total
    full = lax.psum(scaled, ("ka", "cfg"))
    average_rows = lax.dynamic_slice_in_dim(full, row_start, owner_rows_n, 2)
    moment_avg = jnp.stack(
        [to_moment(full[energy], cosine, sine_tab) for energy in range(ENERGIES)]
    )
    correct_list = []
    for energy in range(ENERGIES):
        diff_moment = moment_avg[energy] - coarse[energy]
        spread_d = jnp.einsum("xabm,mk->xabk", diff_moment, onehot, precision=HIGH)
        correct_list.append(batch_trace(spread_d, square_list[energy]))
    return (coarse, average_rows, jnp.stack(correct_list))


def solution(mesh):
    placed = (
        P(),
        P(None, None, None, None, ("ka", "cfg")),
        P(("ka", "cfg")),
        P(("ka", "cfg"), None),
        P(("ka", "cfg")),
        P(),
        P(),
    )
    return jax.shard_map(
        per_device,
        mesh=mesh,
        in_specs=placed,
        out_specs=(P(), P(None, None, "cfg", None), P(None, None, ("ka", "cfg"))),
        check_vma=False,
    )
```

profile of v0, /device:TPU:1, one launch (start us, length us, event | category | flops | bytes accessed | tf_op | source)
XLA Modules:
  0.0 586.7 jit_solution(113416516948212416)
XLA Ops:
  67.3 3.3 fusion.130
  117.0 3.2 fusion.160
  129.3 69.2 %psum.22 = f32[]{:T(128)} all-reduce(f32[]{:T(128)} %bitcast.100), channel_id=1, replica_groups=mesh['ka'=16,'cfg'=8] {'ka','cfg'}, use_global_device_ids=true, to_apply=%region_2.3 | all-reduce | flops 1 | bytes 8 | tf_op jit(solution)/shard_map/psum | solution.py:143
  202.2 57.4 %all-reduce.3.cloned.1.call-done = f32[2,2,16,16,16]{4,3,2,1,0:T(8,128)} async-done(((f32[2,2,16,16,16]{4,3,2,1,0:T(8,128)}), f32[2,2,16,16,16]{4,3,2,1,0:T(8,128)}) %all-reduce.3.cloned.1.call-update) | async-done | bytes 65552 | tf_op jit(solution)/shard_map/psum | solution.py:143
  260.6 3.2 fusion.62
  273.7 4.8 multiply_bitcast_fusion
  278.5 4.1 copy.450
  288.6 3.2 reshape.1083
  298.4 3.2 fusion.66
  312.4 4.9 multiply_bitcast_fusion.2
  317.3 4.1 copy.448
  327.3 3.4 reshape.1068
  337.3 3.1 reshape.1144
  340.4 3.1 reshape.1143
  378.6 140.3 %all-reduce.5.cloned.1.call-done = f32[2,2,256,256]{2,3,1,0:T(8,128)} async-done(((f32[2,2,256,256]{2,3,1,0:T(8,128)}), f32[2,2,256,256]{2,3,1,0:T(8,128)}) %all-reduce.5.cloned.1.call-update) | async-done | bytes 1048592 | tf_op jit(solution)/shard_map/psum | solution.py:154
  522.7 4.4 convolution_bitcast_fusion.5
  527.1 4.4 convolution_bitcast_fusion.6
  533.5 4.4 convolution_bitcast_fusion.4
  537.9 4.4 convolution_bitcast_fusion.7
  544.1 4.4 convolution_bitcast_fusion.9
  548.5 3.7 convolution_bitcast_fusion.10
  552.8 4.4 convolution_bitcast_fusion.8
  557.2 3.9 convolution_bitcast_fusion.11
  570.9 5.1 multiply_reduce_fusion.2
  (356 shorter events, 220.7 us)
Async XLA Ops:
  7.2 252.4 %all-reduce.3.cloned.1.call-start = ((), (), s32[]{:S(2)}) async-start(), calls=%async_computation | async-start | bytes 1048576 | tf_op jit(solution)/shard_map/psum | solution.py:143
  93.6 7.0 %copy-start.23 = (f32[128,16,16]{2,1,0:T(8,128)S(1)}, f32[128,16,16]{2,1,0:T(8,128)}, u32[]{:S(2)}) copy-start(f32[128,16,16]{2,1,0:T(8,128)} %fusion.142) | copy-start | bytes 393220
  96.5 5.1 copy-start.24
  101.6 5.9 %copy-start.26 = (f32[128,16,16]{2,1,0:T(8,128)S(1)}, f32[128,16,16]{2,1,0:T(8,128)}, u32[]{:S(2)}) copy-start(f32[128,16,16]{2,1,0:T(8,128)} %fusion.137) | copy-start | bytes 393220
  103.1 5.5 copy-start.25
  104.9 4.2 copy-start.27
  110.8 408.1 %all-reduce.5.cloned.1.call-start = ((), (), s32[]{:S(2)}) async-start(), calls=%async_computation.1 | async-start | bytes 2097152 | tf_op jit(solution)/shard_map/psum | solution.py:154
  116.3 9.6 %copy-start.6 = (f32[16,16,128]{0,1,2:T(8,128)}, f32[16,16,128]{0,1,2:T(8,128)S(1)}, u32[]{:S(2)}) copy-start(f32[16,16,128]{0,1,2:T(8,128)S(1)} %copy.359) | copy-start | bytes 393220
  116.8 9.1 %copy-start.2 = (f32[16,16,128]{1,0,2:T(8,128)}, f32[16,16,128]{1,0,2:T(8,128)S(1)}, u32[]{:S(2)}) copy-start(f32[16,16,128]{1,0,2:T(8,128)S(1)} %copy.360) | copy-start | bytes 393220
  202.0 63.6 %copy-start.33 = (f32[16,16,16]{2,0,1:T(8,128)}, f32[16,16,16]{2,0,1:T(8,128)S(1)}, u32[]{:S(2)}) copy-start(f32[16,16,16]{2,0,1:T(8,128)S(1)} %copy.323) | copy-start | bytes 49156
  260.6 13.1 %copy-start.20 = (f32[2,2,16,16,16]{4,3,2,1,0:T(8,128)}, f32[2,2,16,16,16]{4,3,2,1,0:T(8,128)S(1)}, u32[]{:S(2)}) copy-start(f32[2,2,16,16,16]{4,3,2,1,0:T(8,128)S(1)} %broadcast_multiply_fusion) | copy-start | bytes 196612
  337.2 6.2 %copy-start.47 = (f32[1,1,256,256]{3,2,1,0:T(8,128)S(1)}, f32[1,1,256,256]{3,2,1,0:T(8,128)}, u32[]{:S(2)}) copy-start(f32[1,1,256,256]{3,2,1,0:T(8,128)} %stack.235) | copy-start | bytes 786436
  337.3 6.2 %copy-start.37 = (f32[16,16,256]{2,1,0:T(8,128)S(1)}, f32[16,16,256]{2,1,0:T(8,128)}, u32[]{:S(2)}) copy-start(f32[16,16,256]{2,1,0:T(8,128)} %reshape.1083) | copy-start | bytes 786436
  355.2 5.2 copy-start.45
  355.2 5.2 copy-start.35
  552.8 8.3 %copy-start.39 = (f32[2,2,256,256]{2,3,1,0:T(8,128)S(1)}, f32[2,2,256,256]{2,3,1,0:T(8,128)}, u32[]{:S(2)}) copy-start(f32[2,2,256,256]{2,3,1,0:T(8,128)} %all-reduce.5.cloned.1.call-done) | copy-start | bytes 3145732
  557.2 5.0 copy-start.56
  566.6 4.2 copy-start.8
  566.6 4.2 copy-start.18
  570.8 5.2 copy-start.7
  570.8 5.2 copy-start.29
  570.8 5.2 copy-start.30
  570.8 5.2 copy-start.31
  570.8 5.2 copy-start.32
  (47 other events, 104.4 us)
Sparse Core Ops, SparseCore 0:
  111.0 148.5 all-reduce.2
  372.9 145.9 all-reduce.4
where the time goes:
time: 597 us; the launch traced here: 587 us
  waiting for transfers between devices  198 us (33%)
  matrix products  166 us (28%)
  local copies, waits for them, and re-layouts  125 us (21%)
  blocking collectives  69.2 us (12%)
  between operations  16.7 us (3%)
  other arithmetic  11.8 us (2%)
    psum x1, waiting for transfers between devices, per_device(): full = lax.psum(scaled, ('ka', 'cfg'))  140 us
    dot_general x32, matrix products, single(): return jnp.einsum('abk,bck->ack', left_m, right_m, precision=HIGH)  83.2 us
    psum x1, blocking collectives, per_device(): lax.psum((jnp.stack(partial_list), jnp.sum(cfg_weight)), ('ka', 'cfg'))  69.2 us
    psum x1, waiting for transfers between devices, per_device(): lax.psum((jnp.stack(partial_list), jnp.sum(cfg_weight)), ('ka', 'cfg'))  57.4 us
    another operation x14, local copies, waits for them, and re-layouts, to_cluster(): jnp.stack([real_part.reshape(order_n, order_n), imag_part.reshape(order_n...  34.7 us
    dot_general x8, matrix products, apply_phase(): return jnp.einsum('mij,iajb->abm', table, block, precision=HIGH)  33.8 us
    dot_general x8, matrix products, apply_phase(): return jnp.einsum('mij,abm->iajb', table, block, precision=HIGH)  24.2 us
    dot_general x16, local copies, waits for them, and re-layouts, single(): return jnp.einsum('abk,bck->ack', left_m, right_m, precision=HIGH)  22.3 us
  transfers between devices with their start and end apart: 2, of which 2 were waited for; matrix products, arithmetic and copies ran while one was open for 5% of the time, Pallas kernels for 0%

commit v1 on v0

v1 whole, which is shorter than its diff:
```python
import functools

import jax
import jax.numpy as jnp
from jax import lax
from jax.experimental import pallas as pl
from jax.experimental.pallas import tpu as pltpu
from jax.sharding import PartitionSpec as P

MESH = pl.DeviceIdType.MESH
F32 = jnp.float32
BF16 = jnp.bfloat16
NN = (((1,), (0,)), ((), ()))
NT = (((1,), (1,)), ((), ()))

ENERGIES = 2
SITES = 16
CHANS = 16
MOMS = 16
WIDE = SITES * CHANS
LANES = 128
ALPHA = 24


def split(x):
    high = x.astype(BF16)
    return high, (x - high.astype(F32)).astype(BF16)


def dot(left, right, dims=NN):
    return lax.dot_general(left, right, dims, preferred_element_type=F32)


def dot_exact(x, right, dims=NN):
    high, low = split(x)
    return dot(high, right, dims) + dot(low, right, dims)


def dot3(x, right, dims=NN):
    high, low = split(x)
    return dot(high, right[0], dims) + (dot(low, right[0], dims) + dot(high, right[1], dims))


def cdot(x, right, dims=NN):
    rows = x[0].shape[0]
    both = jnp.concatenate([x[0], x[1]], axis=0)
    by_re = dot3(both, right[0], dims)
    by_im = dot3(both, right[1], dims)
    return by_re[:rows] - by_im[rows:], by_im[:rows] + by_re[rows:]


def csplit(x):
    return split(x[0]), split(x[1])


def iota(shape, axis):
    return lax.broadcasted_iota(jnp.int32, shape, axis)


def tile_rows(x, times):
    return jnp.concatenate([x] * times, axis=0)


def quarter_turns(mom, site):
    half = site >> 3
    x = 2 * ((site >> 2) & 1) + half
    y = 2 * ((site >> 1) & 1) + half
    z = 2 * (site & 1) + half
    return ((mom >> 2) * x + ((mom >> 1) & 1) * y + (mom & 1) * z) & 3


def cos_sin(turns):
    sign = (1 - (turns & 2)).astype(F32)
    odd = (turns & 1) == 1
    return jnp.where(odd, 0.0, sign), jnp.where(odd, sign, 0.0)


def site_sum(first, second):
    carry = (first & second) >> 3
    return (first ^ second) ^ (7 * carry)


class Tables:
    def __init__(self):
        rows, cols = iota((WIDE, WIDE), 0), iota((WIDE, WIDE), 1)
        self.row_block, self.col_block = rows >> 4, cols >> 4
        self.row_in, self.col_in = rows & 15, cols & 15
        self.same_block = self.row_block == self.col_block
        self.same_in = self.row_in == self.col_in
        self.cos, self.sin = cos_sin(quarter_turns(self.col_block, self.row_block))
        self.wave_cos = jnp.where(self.same_in, self.cos, 0.0).astype(BF16)
        self.wave_sin = jnp.where(self.same_in, self.sin, 0.0).astype(BF16)
        small_r, small_c = iota((SITES, WIDE), 0), iota((SITES, WIDE), 1)
        self.pick_in = (small_r == (small_c & 15)).astype(F32).astype(BF16)
        self.pick_block = (small_r == (small_c >> 4)).astype(F32).astype(BF16)


def block_diag(panel, tab):
    def spread(part):
        return jnp.where(tab.same_block, tile_rows(part.astype(F32), SITES), 0.0).astype(BF16)

    high, low = split(panel)
    return spread(high), spread(low)


def block_diag_c(panel, tab):
    return block_diag(panel[0], tab), block_diag(panel[1], tab)


def kpoint_mul(store, left, right, times=(1.0,)):
    def body(a, carry):
        re = jnp.zeros((CHANS, LANES), F32)
        im = jnp.zeros((CHANS, LANES), F32)
        for b in range(CHANS):
            lr = left[0, a, pl.ds(b, 1), :]
            li = left[1, a, pl.ds(b, 1), :]
            rr = right[0, b]
            ri = right[1, b]
            re = re + (lr * rr - li * ri)
            im = im + (lr * ri + li * rr)
        store(a, re, im)
        return carry

    lax.fori_loop(0, CHANS, body, 0)


def spread_medium(medium, kmap, spread):
    onehot = (iota((MOMS, LANES), 0) == kmap[...]).astype(F32).astype(BF16)
    for e in range(ENERGIES):
        for c in range(2):
            flat = medium[e, c].reshape(WIDE, MOMS)
            spread[e, c] = dot_exact(flat, onehot).reshape(CHANS, CHANS, LANES)


def kpoint_sums(structure, spread, factor, inner, kmap, write_tile):
    for e in range(ENERGIES):
        y, g, f, h = spread.at[e], structure.at[e], factor.at[e], inner.at[e]

        def put_f(a, re, im, f=f):
            f[0, a] = re
            f[1, a] = im

        def put_h(a, re, im, h=h, g=g):
            h[0, a] = g[0, a] + re
            h[1, a] = g[1, a] + im

        kpoint_mul(put_f, y, g)
        kpoint_mul(put_h, g, f)
    rows, lanes = iota((WIDE, LANES), 0), kmap[...]
    onehot_t = ((rows >> 4) == lanes).astype(F32).astype(BF16)
    row_block = iota((WIDE, WIDE), 0) >> 4
    col_in = iota((WIDE, WIDE), 1) & 15
    keep = row_block == col_in
    for e in range(ENERGIES):
        for c in range(2):
            flat = inner[e, c].reshape(WIDE, LANES)
            by_mom = jnp.where(keep, dot_exact(flat, onehot_t, NT), 0.0)
            panel = jnp.sum(by_mom.reshape(CHANS, CHANS, WIDE), axis=0)
            for half in range(2):
                for side in range(2):
                    write_tile(
                        ((e * 2 + c) * 2 + half) * 2 + side,
                        panel[half * 8 : half * 8 + 8, side * LANES : side * LANES + LANES],
                    )


def kpoint_squares(spread, factor, tau, square):
    for e in range(ENERGIES):
        y, f, t, s = spread.at[e], factor.at[e], tau.at[e], square.at[e]

        def put_q(a, re, im, s=s, f=f):
            s[0, a] = f[0, a] + re
            s[1, a] = f[1, a] + im

        def put_t(a, re, im, t=t, y=y):
            t[0, a] = y[0, a] + re
            t[1, a] = y[1, a] + im

        def put_s(a, re, im, s=s):
            s[0, a] = re
            s[1, a] = im

        kpoint_mul(put_q, f, f)
        kpoint_mul(put_t, s, y)
        kpoint_mul(put_s, t, t)


def config_row(occupation, weight, row):
    lane = iota((8, LANES), 1)
    row[...] = jnp.where(lane == SITES, 1.0, 0.0) + jnp.where(
        lane == SITES + 1, weight[0], 0.0
    )
    row[:, 0:SITES] = jnp.broadcast_to(occupation[...].astype(F32), (8, SITES))


def moment_tables(configs, tab, rows_tab, shift_tab):
    turned = jnp.transpose(configs)
    count = turned[0:ALPHA]
    weight = turned[SITES + 1 : SITES + 2]
    weight = weight / jnp.sum(weight, axis=1, keepdims=True)
    live = iota((ALPHA, LANES), 0) <= SITES
    count = jnp.where(live, count, 0.0)
    weighted = count * weight
    flat = configs.astype(BF16)
    lane_r, lane_c = iota((LANES, WIDE), 0), iota((LANES, WIDE), 1)
    pick = (lane_r == (lane_c >> 4)).astype(F32).astype(BF16)
    wide = dot(flat, pick).astype(BF16)
    ones = jnp.ones((LANES, LANES), BF16)
    for s in range(SITES + 1):
        product = weighted * count[s : s + 1]
        rows_tab[s, :, 0:WIDE] = dot_exact(product, wide)
        rows_tab[s, :, WIDE : WIDE + LANES] = dot_exact(product, ones)
    r, c = iota((WIDE, LANES), 0), iota((WIDE, LANES), 1)
    move = (site_sum(r >> 4, r & 15) == c).astype(F32).astype(BF16)
    moved = dot(move, flat, NT)
    moved_b = moved.astype(BF16)
    own = dot(((r >> 4) == c).astype(F32).astype(BF16), flat, NT)
    base = moved * (weight * (1.0 / SITES))
    fold = (tab.row_in == tab.col_block).astype(F32).astype(BF16)
    for which, left in ((0, base), (1, base * own)):
        full = dot_exact(left, moved_b, NT)
        kept = jnp.where(tab.same_block, full, 0.0)
        small = jnp.sum(kept.reshape(SITES, SITES, WIDE), axis=0)
        lanes = dot_exact(small, fold)
        shift_tab[which] = jnp.broadcast_to(
            lanes[:, None, :], (SITES, CHANS, WIDE)
        ).reshape(WIDE, WIDE)


def medium_panels(medium, tab, e):
    out = []
    for c in range(2):
        flat = medium[e, c].reshape(WIDE, MOMS)
        pick = ((iota((MOMS, WIDE), 1) >> 4) == iota((MOMS, WIDE), 0)).astype(F32).astype(BF16)
        by_mom = jnp.where(tab.same_in, dot_exact(flat, pick), 0.0)
        out.append(jnp.sum(by_mom.reshape(CHANS, CHANS, WIDE), axis=1))
    return tuple(out)


def shift_panels(shift_a, shift_b, tab, e):
    def wide(x):
        return dot_exact(x, tab.pick_in)

    b = (wide(shift_b[e, 0]), wide(shift_b[e, 1]))
    c = (
        wide(shift_a[e, 0] - shift_b[e, 0]),
        wide(shift_a[e, 1] - shift_b[e, 1]),
    )
    return b, c


def coarse_panel(y, sum_t, tab, per_moment):
    left = cdot(y, block_diag_c(sum_t, tab), NT)
    both = cdot(left, block_diag_c(y, tab))
    scale = 1.0 / per_moment
    return y[0] + scale * both[0], y[1] + scale * both[1]


def cluster_matrix(x, tab):
    re, im = tile_rows(x[0], SITES), tile_rows(x[1], SITES)
    scale = 1.0 / SITES
    left_r = (re * tab.cos - im * tab.sin) * scale
    left_i = (re * tab.sin + im * tab.cos) * scale
    real = dot_exact(left_r, tab.wave_cos, NT) + dot_exact(left_i, tab.wave_sin, NT)
    imag = dot_exact(left_i, tab.wave_cos, NT) - dot_exact(left_r, tab.wave_sin, NT)
    return real, imag


def rows_stage(cluster, t_parts, b_parts, c_parts, rows_tab, site0, chan):
    def own(ref):
        first = ref[pl.ds(site0 * CHANS + chan, 1), :]
        second = ref[pl.ds((site0 + 1) * CHANS + chan, 1), :]
        return jnp.concatenate(
            [jnp.broadcast_to(first, (8, WIDE)), jnp.broadcast_to(second, (8, WIDE))], axis=0
        )

    start = (own(cluster[0]), own(cluster[1]))
    with_b = cdot(start, b_parts)
    with_c = cdot(start, c_parts)
    row = iota((ALPHA, WIDE), 0)
    block = iota((ALPHA, WIDE), 1) >> 4

    def opened(c):
        out = []
        for at in (0, 8):
            ub = jnp.broadcast_to(with_b[c][at : at + 1], (ALPHA, WIDE))
            uc = jnp.broadcast_to(with_c[c][at : at + 1], (ALPHA, WIDE))
            out.append(jnp.where(row == block, uc, jnp.where(row == SITES, ub, 0.0)))
        return jnp.concatenate(out, axis=0)

    hop = cdot((opened(0), opened(1)), t_parts)
    plain, dressed = [[], []], [[], []]
    for c in range(2):
        for site in range(2):
            f = jnp.zeros((ALPHA, WIDE), F32)
            h = jnp.zeros((ALPHA, WIDE), F32)
            for s in range(SITES + 1):
                line = hop[c][site * ALPHA + s : site * ALPHA + s + 1]
                pair = rows_tab[s, :, WIDE : WIDE + LANES]
                f = f + jnp.concatenate([pair, pair], axis=1) * line
                h = h + rows_tab[s, :, 0:WIDE] * line
            plain[c].append(f)
            dressed[c].append(h)
    plain = tuple(jnp.concatenate(p, axis=0) for p in plain)
    dressed = tuple(jnp.concatenate(d, axis=0) for d in dressed)
    by_b = cdot(plain, b_parts)
    by_c = cdot(dressed, c_parts)
    inner = (by_b[0] + by_c[0], by_b[1] + by_c[1])
    second = cdot(inner, t_parts)
    mean = rows_tab[SITES, SITES : SITES + 1, 0:WIDE]

    def eight(parts):
        return jnp.concatenate([jnp.broadcast_to(p, (8, WIDE)) for p in parts], axis=0)

    for_b, for_c, rest = [], [], []
    for c in range(2):
        last_b, last_c, known = [], [], []
        for site in range(2):
            lines = second[c][site * ALPHA : site * ALPHA + ALPHA]
            picked = jnp.sum(jnp.where(row == block, lines, 0.0), axis=0, keepdims=True)
            last_b.append(lines[SITES : SITES + 1])
            last_c.append(picked)
            known.append(
                with_b[c][site * 8 : site * 8 + 1]
                + with_c[c][site * 8 : site * 8 + 1] * mean
                - inner[c][site * ALPHA + SITES : site * ALPHA + SITES + 1]
            )
        for_b.append(eight(last_b))
        for_c.append(eight(last_c))
        rest.append(eight(known))
    by_b = cdot(tuple(for_b), b_parts)
    by_c = cdot(tuple(for_c), c_parts)
    z = (rest[0] + by_b[0] + by_c[0], rest[1] + by_b[1] + by_c[1])
    last = cdot(z, t_parts)
    return start[0] - last[0], start[1] - last[1]


def moment_stage(cluster, t_parts, x, x_parts, b_wide, c_wide, b_parts, c_parts, shift_tab, tab):
    top = (cluster[0][0:CHANS, :], cluster[1][0:CHANS, :])
    top_parts = csplit(top)

    def head(wide):
        return wide[0][:, 0:CHANS], wide[1][:, 0:CHANS]

    b_in, c_in = head(b_wide), head(c_wide)
    small = (
        jnp.concatenate([b_in[0], c_in[0]], axis=0),
        jnp.concatenate([b_in[1], c_in[1]], axis=0),
    )
    lead = cdot(small, top_parts)
    lead_b = (lead[0][0:CHANS], lead[1][0:CHANS])
    lead_c = (lead[0][CHANS:], lead[1][CHANS:])
    then_b = cdot(lead, b_parts)
    then_c = cdot(lead, c_parts)
    two = shift_tab[1, 0:1, :]
    mean = shift_tab[1, 0:1, 0:1]

    def mix(c):
        bb, cb = then_b[c][0:CHANS], then_b[c][CHANS:]
        bc, cc = then_c[c][0:CHANS], then_c[c][CHANS:]
        return bb + mean * (bc + cb) + two * cc, bb, cb

    re, im = mix(0), mix(1)
    hop = cdot((jnp.concatenate(re, axis=0), jnp.concatenate(im, axis=0)), t_parts)

    def scaled(which):
        return (
            split(cluster[0][...] * shift_tab[which]),
            split(cluster[1][...] * shift_tab[which]),
        )

    pair = cdot((then_c[0][0:CHANS], then_c[1][0:CHANS]), scaled(0))
    triple = cdot((then_c[0][CHANS:], then_c[1][CHANS:]), scaled(1))
    for_b, for_c = [], []
    for c in range(2):
        h = hop[c]
        for_b.append(h[0:CHANS] - (lead_b[c] + mean * lead_c[c]))
        for_c.append(
            mean * h[CHANS : 2 * CHANS]
            + two * h[2 * CHANS : 3 * CHANS]
            + pair[c]
            + triple[c]
            - (mean * lead_b[c] + two * lead_c[c])
        )
    by_b = cdot(tuple(for_b), b_parts)
    by_c = cdot(tuple(for_c), c_parts)
    line_r, line_i = by_b[0] + by_c[0], by_b[1] + by_c[1]
    m_r = dot_exact(line_r, tab.wave_cos) - dot_exact(line_i, tab.wave_sin)
    m_i = dot_exact(line_r, tab.wave_sin) + dot_exact(line_i, tab.wave_cos)
    m_r = m_r + b_wide[0] + mean * c_wide[0]
    m_i = m_i + b_wide[1] + mean * c_wide[1]
    d = cdot(cdot(x, block_diag_c((m_r, m_i), tab)), x_parts)
    return -d[0], -d[1]


def correction_stage(d, square, e, kmap, tab):
    onehot = ((iota((WIDE, LANES), 0) >> 4) == kmap[...]).astype(F32).astype(BF16)
    keep = tab.row_block == tab.col_in

    def spread(panel):
        high, low = split(panel)

        def one(part):
            full = jnp.where(keep, tile_rows(part.astype(F32), CHANS), 0.0)
            return dot(full.astype(BF16), onehot)

        return one(high) + one(low)

    dr, di = spread(d[0]), spread(d[1])
    sr, si = square[e, 0].reshape(WIDE, LANES), square[e, 1].reshape(WIDE, LANES)
    re = jnp.sum(dr * sr - di * si, axis=0, keepdims=True)
    im = jnp.sum(dr * si + di * sr, axis=0, keepdims=True)
    return re, im


def coarse_out(x, tab, store):
    fold = (tab.col_block == tab.row_in)
    pick = (iota((WIDE, MOMS), 0) >> 4 == iota((WIDE, MOMS), 1)).astype(F32).astype(BF16)
    high = x.astype(BF16)
    rest = x - high.astype(F32)
    mid = rest.astype(BF16)
    low = (rest - mid.astype(F32)).astype(BF16)
    total = None
    for part in (low, mid, high):
        wide = jnp.broadcast_to(part.astype(F32)[:, None, :], (CHANS, CHANS, WIDE))
        wide = jnp.where(tab.same_in, wide.reshape(WIDE, WIDE), 0.0).astype(BF16)
        piece = dot(wide, pick)
        total = piece if total is None else total + piece
    store(total.reshape(CHANS, CHANS, MOMS))


def gathered_panel(tiles, at):
    top = jnp.concatenate([tiles[at], tiles[at + 1]], axis=1)
    low = jnp.concatenate([tiles[at + 2], tiles[at + 3]], axis=1)
    return jnp.concatenate([top, low], axis=0)


def kpoint_kernel(structure, medium, kmap, occupation, weight, sums, row, square, spread, factor, inner):
    spread_medium(medium, kmap, spread)

    def write(at, value):
        sums[at] = value

    kpoint_sums(structure, spread, factor, inner, kmap, write)
    config_row(occupation, weight, row)
    kpoint_squares(spread, factor, inner, square)


def reduce_kernel(
    n_ka, n_cfg, sums, row, total, configs,
    outgoing, first, own_rows, part, rows_send, rows_recv, a_send, a_recv, b_send, b_recv, c_send, c_recv,
):
    ka, cfg = lax.axis_index("ka"), lax.axis_index("cfg")
    barrier = pltpu.get_barrier_semaphore()
    for d in range(1, n_ka):
        pl.semaphore_signal(barrier, inc=1, device_id=(lax.rem(ka + d, n_ka), cfg), device_id_type=MESH)
    for d in range(1, n_cfg):
        pl.semaphore_signal(barrier, inc=1, device_id=(ka, lax.rem(cfg + d, n_cfg)), device_id_type=MESH)
    pl.semaphore_wait(barrier, n_ka + n_cfg - 2)

    def cfg_copy(src, slots, send, recv, d):
        return pltpu.make_async_remote_copy(
            src_ref=src, dst_ref=slots.at[cfg], send_sem=send.at[d], recv_sem=recv.at[cfg],
            device_id=(ka, lax.rem(cfg + d, n_cfg)), device_id_type=MESH,
        )

    def cfg_wait(src, slots, send, recv, d):
        at = lax.rem(cfg + d, n_cfg)
        pltpu.make_async_remote_copy(
            src_ref=src, dst_ref=slots.at[at], send_sem=send.at[d], recv_sem=recv.at[at],
            device_id=(ka, at), device_id_type=MESH,
        ).wait_recv()

    def ka_copy(src, slots, send, recv, d):
        return pltpu.make_async_remote_copy(
            src_ref=src, dst_ref=slots.at[ka], send_sem=send.at[d], recv_sem=recv.at[ka],
            device_id=(lax.rem(ka + d, n_ka), cfg), device_id_type=MESH,
        )

    def ka_wait(src, slots, send, recv, d):
        at = lax.rem(ka + d, n_ka)
        pltpu.make_async_remote_copy(
            src_ref=src, dst_ref=slots.at[at], send_sem=send.at[d], recv_sem=recv.at[at],
            device_id=(at, cfg), device_id_type=MESH,
        ).wait_recv()

    for d in range(1, n_cfg):
        cfg_copy(row, own_rows, rows_send, rows_recv, d).start()
    own_rows[cfg] = row[...]
    for d in range(1, n_cfg):
        cfg_wait(row, own_rows, rows_send, rows_recv, d)
    line = iota((8, LANES), 0)
    group = jnp.zeros((8, LANES), F32)
    for at in range(n_cfg):
        group = group + jnp.where(line == at, own_rows[at], 0.0)
    for at in range(n_ka):
        outgoing[at, 0] = sums[at]
        outgoing[at, 1] = group
    for d in range(1, n_ka):
        ka_copy(outgoing.at[lax.rem(ka + d, n_ka)], first, a_send, a_recv, d).start()
    first[ka] = outgoing[ka]
    for d in range(1, n_ka):
        ka_wait(outgoing.at[0], first, a_send, a_recv, d)
    value = first[0, 0]
    configs[0] = first[0, 1]
    for at in range(1, n_ka):
        value = value + first[at, 0]
        configs[at] = first[at, 1]
    part[cfg] = value
    for d in range(1, n_cfg):
        cfg_copy(part.at[cfg], part, b_send, b_recv, d).start()
    for d in range(1, n_cfg):
        cfg_wait(part.at[cfg], part, b_send, b_recv, d)
    value = part[0]
    for at in range(1, n_cfg):
        value = value + part[at]
    total[ka] = value
    for d in range(1, n_ka):
        ka_copy(total.at[ka], total, c_send, c_recv, d).start()
    for d in range(1, n_ka):
        ka_wait(total.at[ka], total, c_send, c_recv, d)
    for d in range(1, n_cfg):
        cfg_copy(row, own_rows, rows_send, rows_recv, d).wait_send()
        cfg_copy(part.at[cfg], part, b_send, b_recv, d).wait_send()
    for d in range(1, n_ka):
        ka_copy(outgoing.at[0], first, a_send, a_recv, d).wait_send()
        ka_copy(total.at[ka], total, c_send, c_recv, d).wait_send()


def cluster_kernel(
    per_moment, total, configs, medium, kmap, shift_a, shift_b, square, coarse, block, correction,
    cluster, rows_tab, shift_tab,
):
    ka, cfg = lax.axis_index("ka"), lax.axis_index("cfg")
    cluster_body(
        per_moment, ka, cfg, total, configs, medium, kmap, shift_a, shift_b, square, coarse, block,
        correction, cluster, rows_tab, shift_tab,
    )


def cluster_body(
    per_moment, ka, cfg, total, configs, medium, kmap, shift_a, shift_b, square, coarse, block, correction,
    cluster, rows_tab, shift_tab,
):
    tab = Tables()
    moment_tables(configs[...].reshape(LANES, LANES), tab, rows_tab, shift_tab)
    which = iota((8, WIDE), 0)
    out = jnp.zeros((8, WIDE), F32)
    for e in range(ENERGIES):
        y = medium_panels(medium, tab, e)
        b_wide, c_wide = shift_panels(shift_a, shift_b, tab, e)
        b_parts, c_parts = block_diag_c(b_wide, tab), block_diag_c(c_wide, tab)
        sum_t = (gathered_panel(total, e * 8), gathered_panel(total, e * 8 + 4))
        x = coarse_panel(y, sum_t, tab, per_moment)
        x_parts = block_diag_c(x, tab)
        real, imag = cluster_matrix(x, tab)
        cluster[e, 0] = real
        cluster[e, 1] = imag
        t_parts = split(real), split(imag)
        held = (cluster.at[e, 0], cluster.at[e, 1])
        avg = rows_stage(held, t_parts, b_parts, c_parts, rows_tab, cfg * 2, ka)
        for c in range(2):
            for site in range(2):
                at = e * 4 + c * 2 + site
                out = jnp.where(which == at, avg[c][site * 8 : site * 8 + 8], out)
        d = moment_stage(
            held, t_parts, x, x_parts, b_wide, c_wide, b_parts, c_parts, shift_tab, tab
        )
        re, im = correction_stage(d, square, e, kmap, tab)
        correction[e, 0:1, :] = re
        correction[e, 1:2, :] = im
        for c in range(2):
            def store(value, e=e, c=c):
                coarse[e, c] = value

            coarse_out(x[c], tab, store)
    block[...] = out


def gather_kernel(n_ka, block, average, slots, send, recv):
    ka, cfg = lax.axis_index("ka"), lax.axis_index("cfg")
    barrier = pltpu.get_barrier_semaphore()
    for d in range(1, n_ka):
        pl.semaphore_signal(barrier, inc=1, device_id=(lax.rem(ka + d, n_ka), cfg), device_id_type=MESH)
    pl.semaphore_wait(barrier, n_ka - 1)

    def copy(at, d):
        return pltpu.make_async_remote_copy(
            src_ref=block, dst_ref=slots.at[at], send_sem=send.at[d], recv_sem=recv.at[at],
            device_id=(lax.rem(ka + d, n_ka), cfg), device_id_type=MESH,
        )

    for d in range(1, n_ka):
        copy(ka, d).start()
    slots[ka] = block[...]
    for d in range(1, n_ka):
        copy(lax.rem(ka + d, n_ka), d).wait_recv()
    for at in range(n_ka):
        for e in range(ENERGIES):
            for c in range(2):
                for site in range(2):
                    line = e * 4 + c * 2 + site
                    row = site * CHANS + at
                    average[e, c, row : row + 1, :] = slots[at, line : line + 1, :]
    for d in range(1, n_ka):
        copy(ka, d).wait_send()


def shape(*dims):
    return jax.ShapeDtypeStruct(dims, F32)


VMEM_SPEC = pl.BlockSpec(memory_space=pltpu.VMEM)
SMEM_SPEC = pl.BlockSpec(memory_space=pltpu.SMEM)


def per_device(medium_t, structure, kmap, occupation, cfg_weight, shift_a, shift_b):
    n_ka, n_cfg = lax.axis_size("ka"), lax.axis_size("cfg")
    per_moment = kmap.shape[0] * n_ka * n_cfg // MOMS
    kmap = kmap.reshape(1, LANES)
    kdims = (ENERGIES, 2, CHANS, CHANS, LANES)
    params = functools.partial(pltpu.CompilerParams, vmem_limit_bytes=48 * 1024 * 1024)
    sums, row, square = pl.pallas_call(
        kpoint_kernel,
        out_shape=(shape(16, 8, LANES), shape(8, LANES), shape(*kdims)),
        in_specs=[VMEM_SPEC] * 4 + [SMEM_SPEC],
        out_specs=(VMEM_SPEC,) * 3,
        scratch_shapes=[pltpu.VMEM(kdims, F32)] * 3,
        compiler_params=params(),
    )(structure, medium_t, kmap, occupation, cfg_weight)
    dma = pltpu.SemaphoreType.DMA
    total, configs = pl.pallas_call(
        functools.partial(reduce_kernel, n_ka, n_cfg),
        out_shape=(shape(16, 8, LANES), shape(16, 8, LANES)),
        in_specs=[VMEM_SPEC] * 2,
        out_specs=(VMEM_SPEC,) * 2,
        scratch_shapes=[
            pltpu.VMEM((n_ka, 2, 8, LANES), F32),
            pltpu.VMEM((n_ka, 2, 8, LANES), F32),
            pltpu.VMEM((n_cfg, 8, LANES), F32),
            pltpu.VMEM((n_cfg, 8, LANES), F32),
            dma((n_cfg,)), dma((n_cfg,)),
            dma((n_ka,)), dma((n_ka,)),
            dma((n_cfg,)), dma((n_cfg,)),
            dma((n_ka,)), dma((n_ka,)),
        ],
        compiler_params=params(collective_id=0, has_side_effects=True),
    )(sums, row)
    coarse, block, correction = pl.pallas_call(
        functools.partial(cluster_kernel, per_moment),
        out_shape=(
            shape(ENERGIES, 2, CHANS, CHANS, MOMS),
            shape(8, WIDE),
            shape(ENERGIES, 2, LANES),
        ),
        in_specs=[VMEM_SPEC] * 7,
        out_specs=(VMEM_SPEC,) * 3,
        scratch_shapes=[
            pltpu.VMEM((ENERGIES, 2, WIDE, WIDE), F32),
            pltpu.VMEM((SITES + 1, ALPHA, WIDE + LANES), F32),
            pltpu.VMEM((2, WIDE, WIDE), F32),
        ],
        compiler_params=params(),
    )(total, configs, medium_t, kmap, shift_a, shift_b, square)
    average = pl.pallas_call(
        functools.partial(gather_kernel, n_ka),
        out_shape=shape(ENERGIES, 2, 2 * CHANS, WIDE),
        in_specs=[VMEM_SPEC],
        out_specs=VMEM_SPEC,
        scratch_shapes=[pltpu.VMEM((n_ka, 8, WIDE), F32), dma((n_ka,)), dma((n_ka,))],
        compiler_params=params(collective_id=1, has_side_effects=True),
    )(block)
    return coarse, average, correction


def solution(mesh):
    placed = (
        P(),
        P(None, None, None, None, ("ka", "cfg")),
        P(("ka", "cfg")),
        P(("ka", "cfg"), None),
        P(("ka", "cfg")),
        P(),
        P(),
    )
    return jax.shard_map(
        per_device,
        mesh=mesh,
        in_specs=placed,
        out_specs=(P(), P(None, None, "cfg", None), P(None, None, ("ka", "cfg"))),
        check_vma=False,
    )
```

time: 597 us -> 62.9 us (0.11); the launches traced: 587 us -> 61.7 us
  waiting for transfers between devices: 198 us -> 0 us
  matrix products: 166 us -> 0 us
  local copies, waits for them, and re-layouts: 125 us -> 3.41 us
  blocking collectives: 69.2 us -> 0 us
  Pallas kernels: 0 us -> 56.9 us
  between operations: 16.7 us -> 1.36 us
  other arithmetic: 11.8 us -> 0 us
    psum x2 -> x0, waiting for transfers between devices: 198 us -> none  [the longest x1 140 us: per_device(): full = lax.psum(scaled, ('ka', 'cfg'))]
    dot_general x102 -> x0, matrix products: 166 us -> none  [the longest x32 83.2 us: single(): return jnp.einsum('abk,bck->ack', left_m, right_m, precision=HIGH)]
    psum x1 -> x0, blocking collectives: 69.2 us -> none  [per_device(): lax.psum((jnp.stack(partial_list), jnp.sum(cfg_weight)), ('ka', 'cfg'))]
    another operation x26 -> x0, local copies, waits for them, and re-layouts: 57.4 us -> none  [the longest x14 34.7 us: to_cluster(): jnp.stack([real_part.reshape(order_n, order_n), imag_part.reshape(order_n...]
    pallas_call x0 -> x4, Pallas kernels: none -> 56.9 us  [the longest x1 25.7 us: per_device(): pl.pallas_call(functools.partial(reduce_kernel, n_ka, n_cfg), out_shape=(...]
    dot_general x16 -> x0, local copies, waits for them, and re-layouts: 22.3 us -> none  [single(): return jnp.einsum('abk,bck->ack', left_m, right_m, precision=HIGH)]
    squeeze x18 -> x0, local copies, waits for them, and re-layouts: 13.4 us -> none  [the longest x12 6.78 us: batch_mul(): second_m[0]]
    unnamed x151 -> x15, local copies, waits for them, and re-layouts: 16.5 us -> 3.41 us
  transfers between devices with their start and end apart: 2 -> 0, of which waited for: 2 -> 0; matrix products, arithmetic and copies ran while one was open for 5% -> 0% of each run, Pallas kernels for 0% -> 0%
where the time goes in v1:
time: 62.9 us; the launch traced here: 61.7 us
  Pallas kernels  56.9 us (90%)
  local copies, waits for them, and re-layouts  3.41 us (5%)
  between operations  1.36 us (2%)
    pallas_call x1, Pallas kernels, per_device(): pl.pallas_call(functools.partial(reduce_kernel, n_ka, n_cfg), out_shape=(...  25.7 us
    pallas_call x1, Pallas kernels, per_device(): pl.pallas_call(functools.partial(cluster_kernel, per_moment), out_shape=(...  15.8 us
    pallas_call x1, Pallas kernels, per_device(): pl.pallas_call(kpoint_kernel, out_shape=(shape(16, 8, LANES), shape(8, LA...  8.18 us
    pallas_call x1, Pallas kernels, per_device(): pl.pallas_call(functools.partial(gather_kernel, n_ka), out_shape=shape(EN...  7.23 us
    unnamed x15, local copies, waits for them, and re-layouts  3.41 us

profile of v1, /device:TPU:1, one launch (start us, length us, event | category | flops | bytes accessed | tf_op | source)
XLA Modules:
  0.0 61.7 jit_solution(212878333141121323)
XLA Ops:
  1.3 0.0 copy-start.5
  1.3 0.0 copy-start.6
  1.3 0.6 %copy-done.5 = s32[128]{0:T(128)S(1)} copy-done((s32[128]{0:T(128)S(1)}, s32[128]{0:T(128)}, u32[]{:S(2)}) %copy-start.5) | copy-done | bytes 536
  1.9 0.0 copy-done.6
  1.9 0.0 copy-start
  2.0 1.0 %copy-done = f32[2,2,16,16,16]{4,3,2,1,0:T(8,128)S(1)} copy-done((f32[2,2,16,16,16]{4,3,2,1,0:T(8,128)S(1)}, f32[2,2,16,16,16]{4,3,2,1,0:T(8,128)}, u32[]{:S(2)}) %copy-start) | copy-done | bytes 65560
  3.0 0.0 copy-start.2
  3.0 1.0 %copy-done.2 = f32[2,2,16,16,128]{4,3,2,1,0:T(8,128)S(1)} copy-done((f32[2,2,16,16,128]{4,3,2,1,0:T(8,128)S(1)}, f32[2,2,16,16,128]{4,3,2,1,0:T(8,128)}, u32[]{:S(2)}) %copy-start.2) | copy-done | bytes 524312
  4.0 0.0 copy-start.1
  4.0 8.2 %shard_map.94 = (f32[16,8,128]{2,1,0:T(8,128)S(1)}, f32[8,128]{1,0:T(8,128)S(1)}, f32[2,2,16,16,128]{4,3,2,1,0:T(8,128)S(1)}) custom-call(f32[2,2,16,16,128]{4,3,2,1,0:T(8,128)S(1)} %copy-done.2, f32[2,2,16,16,16]{4,3,2,1,0:T(8,128)S(1)} %copy-done, s32[1,128]{1,0:T(1,128)S(1)} %bitcast.1, s32[1,16]{1,0:T(1,128)S(1)} %copy-done.6, f32[1]{0:T(128)S(6)} %copy.11.weight), custom_call_target="tpu_custom_call" | custom-call | tf_op jit(solution)/shard_map/pallas_call | solution.py:623
  12.2 0.0 copy-start.3
  12.2 0.0 copy-start.4
  12.2 25.7 %shard_map.95 = (f32[16,8,128]{2,1,0:T(8,128)S(1)}, f32[16,8,128]{2,1,0:T(8,128)S(1)}) custom-call(f32[16,8,128]{2,1,0:T(8,128)S(1)} %get-tuple-element.11.sums, f32[8,128]{1,0:T(8,128)S(1)} %get-tuple-element.12.row), custom_call_target="tpu_custom_call" | custom-call | tf_op jit(solution)/shard_map/pallas_call | solution.py:632
  37.9 0.0 copy-done.1
  37.9 0.0 copy-done.3
  38.0 0.0 copy-done.4
  38.0 15.8 %shard_map.96 = (f32[2,2,16,16,16]{4,3,2,1,0:T(8,128)}, f32[8,256]{1,0:T(8,128)S(1)}, f32[2,2,128]{2,1,0:T(2,128)}) custom-call(f32[16,8,128]{2,1,0:T(8,128)S(1)} %get-tuple-element.13.total, f32[16,8,128]{2,1,0:T(8,128)S(1)} %get-tuple-element.14.configs, f32[2,2,16,16,16]{4,3,2,1,0:T(8,128)S(1)} %copy-done.1, s32[1,128]{1,0:T(1,128)S(1)} %bitcast.2, ...), custom_call_target="tpu_custom_call" | custom-call | tf_op jit(solution)/shard_map/pallas_call | solution.py:649
  53.8 7.2 %shard_map.97 = f32[2,2,32,256]{3,2,1,0:T(8,128)S(1)} custom-call(f32[8,256]{1,0:T(8,128)S(1)} %get-tuple-element.17.block), custom_call_target="tpu_custom_call" | custom-call | tf_op jit(solution)/shard_map/pallas_call | solution.py:665
  61.0 0.7 %copy.12 = f32[2,2,32,256]{3,2,1,0:T(8,128)} copy(f32[2,2,32,256]{3,2,1,0:T(8,128)S(1)} %shard_map.97) | data formatting | bytes 262144
Async XLA Ops:
  1.3 0.7 %copy-start.5 = (s32[128]{0:T(128)S(1)}, s32[128]{0:T(128)}, u32[]{:S(2)}) copy-start(s32[128]{0:T(128)} %param.9) | copy-start | bytes 1540
  1.3 0.7 %copy-start.6 = (s32[1,16]{1,0:T(1,128)S(1)}, s32[1,16]{1,0:T(1,128)}, u32[]{:S(2)}) copy-start(s32[1,16]{1,0:T(1,128)} %occupation.1) | copy-start | bytes 196
  1.9 1.0 %copy-start = (f32[2,2,16,16,16]{4,3,2,1,0:T(8,128)S(1)}, f32[2,2,16,16,16]{4,3,2,1,0:T(8,128)}, u32[]{:S(2)}) copy-start(f32[2,2,16,16,16]{4,3,2,1,0:T(8,128)} %medium.3) | copy-start | bytes 196612
  3.0 1.0 %copy-start.2 = (f32[2,2,16,16,128]{4,3,2,1,0:T(8,128)S(1)}, f32[2,2,16,16,128]{4,3,2,1,0:T(8,128)}, u32[]{:S(2)}) copy-start(f32[2,2,16,16,128]{4,3,2,1,0:T(8,128)} %structure.1) | copy-start | bytes 1572868
  4.0 33.9 %copy-start.1 = (f32[2,2,16,16,16]{4,3,2,1,0:T(8,128)S(1)}, f32[2,2,16,16,16]{4,3,2,1,0:T(8,128)}, u32[]{:S(2)}) copy-start(f32[2,2,16,16,16]{4,3,2,1,0:T(8,128)} %medium.3) | copy-start | bytes 196612
  12.2 25.7 %copy-start.3 = (f32[2,2,16,16]{3,2,1,0:T(8,128)S(1)}, f32[2,2,16,16]{3,2,1,0:T(8,128)}, u32[]{:S(2)}) copy-start(f32[2,2,16,16]{3,2,1,0:T(8,128)} %shift_a.1) | copy-start | bytes 12292
  12.2 25.7 %copy-start.4 = (f32[2,2,16,16]{3,2,1,0:T(8,128)S(1)}, f32[2,2,16,16]{3,2,1,0:T(8,128)}, u32[]{:S(2)}) copy-start(f32[2,2,16,16]{3,2,1,0:T(8,128)} %shift_b.1) | copy-start | bytes 12292

commit v2 on v1

--- a/solution.py
+++ b/solution.py
@@ -107,7 +107,7 @@
     return block_diag(panel[0], tab), block_diag(panel[1], tab)
 
 
-def kpoint_mul(store, left, right, times=(1.0,)):
+def kpoint_mul(store, left, right):
     def body(a, carry):
         re = jnp.zeros((CHANS, LANES), F32)
         im = jnp.zeros((CHANS, LANES), F32)
@@ -132,20 +132,22 @@
             spread[e, c] = dot_exact(flat, onehot).reshape(CHANS, CHANS, LANES)
 
 
-def kpoint_sums(structure, spread, factor, inner, kmap, write_tile):
-    for e in range(ENERGIES):
-        y, g, f, h = spread.at[e], structure.at[e], factor.at[e], inner.at[e]
-
-        def put_f(a, re, im, f=f):
-            f[0, a] = re
-            f[1, a] = im
-
-        def put_h(a, re, im, h=h, g=g):
-            h[0, a] = g[0, a] + re
-            h[1, a] = g[1, a] + im
-
-        kpoint_mul(put_f, y, g)
-        kpoint_mul(put_h, g, f)
+def kpoint_inner(structure, spread, factor, inner, e):
+    y, g, f, h = spread.at[e], structure.at[e], factor.at[e], inner.at[e]
+
+    def put_f(a, re, im):
+        f[0, a] = re
+        f[1, a] = im
+
+    def put_h(a, re, im):
+        h[0, a] = g[0, a] + re
+        h[1, a] = g[1, a] + im
+
+    kpoint_mul(put_f, y, g)
+    kpoint_mul(put_h, g, f)
+
+
+def kpoint_sums(inner, kmap, write_tile):
     rows, lanes = iota((WIDE, LANES), 0), kmap[...]
     onehot_t = ((rows >> 4) == lanes).astype(F32).astype(BF16)
     row_block = iota((WIDE, WIDE), 0) >> 4
@@ -249,9 +251,9 @@
     return b, c
 
 
-def coarse_panel(y, sum_t, tab, per_moment):
+def coarse_panel(y, y_parts, sum_t, tab, per_moment):
     left = cdot(y, block_diag_c(sum_t, tab), NT)
-    both = cdot(left, block_diag_c(y, tab))
+    both = cdot(left, y_parts)
     scale = 1.0 / per_moment
     return y[0] + scale * both[0], y[1] + scale * both[1]
 
@@ -435,175 +437,159 @@
     return jnp.concatenate([top, low], axis=0)
 
 
-def kpoint_kernel(structure, medium, kmap, occupation, weight, sums, row, square, spread, factor, inner):
+class Exchange:
+    def __init__(self, axis, count, slots, send, recv):
+        self.axis, self.count = axis, count
+        self.slots, self.send, self.recv = slots, send, recv
+        self.me = lax.axis_index(axis)
+
+    def peer(self, d):
+        return lax.rem(self.me + d, self.count)
+
+    def copy(self, src, at, d):
+        return pltpu.make_async_remote_copy(
+            src_ref=src, dst_ref=self.slots.at[at], send_sem=self.send.at[d],
+            recv_sem=self.recv.at[at], device_id={self.axis: self.peer(d)}, device_id_type=MESH,
+        )
+
+    def start(self, source):
+        for d in range(1, self.count):
+            self.copy(source(self.peer(d)), self.me, d).start()
+
+    def wait(self, source):
+        for d in range(1, self.count):
+            self.copy(source(self.me), self.peer(d), d).wait_recv()
+
+    def drain(self, source):
+        for d in range(1, self.count):
+            self.copy(source(self.me), self.me, d).wait_send()
+
+
+def greet(n_ka, n_cfg):
+    barrier = pltpu.get_barrier_semaphore()
+    for axis, count in (("ka", n_ka), ("cfg", n_cfg)):
+        me = lax.axis_index(axis)
+        for d in range(1, count):
+            pl.semaphore_signal(
+                barrier, inc=1, device_id={axis: lax.rem(me + d, count)}, device_id_type=MESH
+            )
+    return barrier
+
+
+def kernel(
+    per_moment, n_ka, n_cfg,
+    structure_hbm, medium_hbm, kmap, occupation, weight, shift_a, shift_b,
+    coarse, average, correction,
+    structure, medium, spread, factor, inner, square, cluster, rows_tab, shift_tab,
+    row, own_rows, outgoing, first, part, total, block, slots,
+    load_sem, row_send, row_recv, first_send, first_recv, part_send, part_recv,
+    total_send, total_recv, slot_send, slot_recv,
+):
+    barrier = greet(n_ka, n_cfg)
+    loads = [
+        pltpu.make_async_copy(medium_hbm, medium, load_sem.at[0]),
+        pltpu.make_async_copy(structure_hbm, structure, load_sem.at[1]),
+    ]
+    for load in loads:
+        load.start()
+    rows_x = Exchange("cfg", n_cfg, own_rows, row_send, row_recv)
+    first_x = Exchange("ka", n_ka, first, first_send, first_recv)
+    part_x = Exchange("cfg", n_cfg, part, part_send, part_recv)
+    total_x = Exchange("ka", n_ka, total, total_send, total_recv)
+    slot_x = Exchange("ka", n_ka, slots, slot_send, slot_recv)
+    ka, cfg = first_x.me, rows_x.me
+    config_row(occupation, weight, row)
+    loads[0].wait()
     spread_medium(medium, kmap, spread)
+    loads[1].wait()
+    kpoint_inner(structure, spread, factor, inner, 0)
+    pl.semaphore_wait(barrier, n_ka + n_cfg - 2)
+    rows_x.start(lambda to: row)
+    own_rows[cfg] = row[...]
+    kpoint_inner(structure, spread, factor, inner, 1)
 
     def write(at, value):
-        sums[at] = value
-
-    kpoint_sums(structure, spread, factor, inner, kmap, write)
-    config_row(occupation, weight, row)
-    kpoint_squares(spread, factor, inner, square)
-
-
-def reduce_kernel(
-    n_ka, n_cfg, sums, row, total, configs,
-    outgoing, first, own_rows, part, rows_send, rows_recv, a_send, a_recv, b_send, b_recv, c_send, c_recv,
-):
-    ka, cfg = lax.axis_index("ka"), lax.axis_index("cfg")
-    barrier = pltpu.get_barrier_semaphore()
-    for d in range(1, n_ka):
-        pl.semaphore_signal(barrier, inc=1, device_id=(lax.rem(ka + d, n_ka), cfg), device_id_type=MESH)
-    for d in range(1, n_cfg):
-        pl.semaphore_signal(barrier, inc=1, device_id=(ka, lax.rem(cfg + d, n_cfg)), device_id_type=MESH)
-    pl.semaphore_wait(barrier, n_ka + n_cfg - 2)
-
-    def cfg_copy(src, slots, send, recv, d):
-        return pltpu.make_async_remote_copy(
-            src_ref=src, dst_ref=slots.at[cfg], send_sem=send.at[d], recv_sem=recv.at[cfg],
-            device_id=(ka, lax.rem(cfg + d, n_cfg)), device_id_type=MESH,
-        )
-
-    def cfg_wait(src, slots, send, recv, d):
-        at = lax.rem(cfg + d, n_cfg)
-        pltpu.make_async_remote_copy(
-            src_ref=src, dst_ref=slots.at[at], send_sem=send.at[d], recv_sem=recv.at[at],
-            device_id=(ka, at), device_id_type=MESH,
-        ).wait_recv()
-
-    def ka_copy(src, slots, send, recv, d):
-        return pltpu.make_async_remote_copy(
-            src_ref=src, dst_ref=slots.at[ka], send_sem=send.at[d], recv_sem=recv.at[ka],
-            device_id=(lax.rem(ka + d, n_ka), cfg), device_id_type=MESH,
-        )
-
-    def ka_wait(src, slots, send, recv, d):
-        at = lax.rem(ka + d, n_ka)
-        pltpu.make_async_remote_copy(
-            src_ref=src, dst_ref=slots.at[at], send_sem=send.at[d], recv_sem=recv.at[at],
-            device_id=(at, cfg), device_id_type=MESH,
-        ).wait_recv()
-
-    for d in range(1, n_cfg):
-        cfg_copy(row, own_rows, rows_send, rows_recv, d).start()
-    own_rows[cfg] = row[...]
-    for d in range(1, n_cfg):
-        cfg_wait(row, own_rows, rows_send, rows_recv, d)
+        outgoing[at, 0] = value
+
+    kpoint_sums(inner, kmap, write)
+    rows_x.wait(lambda to: row)
     line = iota((8, LANES), 0)
     group = jnp.zeros((8, LANES), F32)
     for at in range(n_cfg):
         group = group + jnp.where(line == at, own_rows[at], 0.0)
     for at in range(n_ka):
-        outgoing[at, 0] = sums[at]
         outgoing[at, 1] = group
-    for d in range(1, n_ka):
-        ka_copy(outgoing.at[lax.rem(ka + d, n_ka)], first, a_send, a_recv, d).start()
+    first_x.start(lambda to: outgoing.at[to])
     first[ka] = outgoing[ka]
-    for d in range(1, n_ka):
-        ka_wait(outgoing.at[0], first, a_send, a_recv, d)
+    kpoint_squares(spread, factor, inner, square)
+    first_x.wait(lambda to: outgoing.at[to])
     value = first[0, 0]
-    configs[0] = first[0, 1]
     for at in range(1, n_ka):
         value = value + first[at, 0]
-        configs[at] = first[at, 1]
     part[cfg] = value
-    for d in range(1, n_cfg):
-        cfg_copy(part.at[cfg], part, b_send, b_recv, d).start()
-    for d in range(1, n_cfg):
-        cfg_wait(part.at[cfg], part, b_send, b_recv, d)
+    part_x.start(lambda to: part.at[cfg])
+    tab = Tables()
+    y = [medium_panels(medium, tab, e) for e in range(ENERGIES)]
+    y_parts = [block_diag_c(y[e], tab) for e in range(ENERGIES)]
+    wide = [shift_panels(shift_a, shift_b, tab, e) for e in range(ENERGIES)]
+    b_parts = [block_diag_c(wide[e][0], tab) for e in range(ENERGIES)]
+    c_parts = [block_diag_c(wide[e][1], tab) for e in range(ENERGIES)]
+    part_x.wait(lambda to: part.at[cfg])
     value = part[0]
     for at in range(1, n_cfg):
         value = value + part[at]
     total[ka] = value
-    for d in range(1, n_ka):
-        ka_copy(total.at[ka], total, c_send, c_recv, d).start()
-    for d in range(1, n_ka):
-        ka_wait(total.at[ka], total, c_send, c_recv, d)
-    for d in range(1, n_cfg):
-        cfg_copy(row, own_rows, rows_send, rows_recv, d).wait_send()
-        cfg_copy(part.at[cfg], part, b_send, b_recv, d).wait_send()
-    for d in range(1, n_ka):
-        ka_copy(outgoing.at[0], first, a_send, a_recv, d).wait_send()
-        ka_copy(total.at[ka], total, c_send, c_recv, d).wait_send()
-
-
-def cluster_kernel(
-    per_moment, total, configs, medium, kmap, shift_a, shift_b, square, coarse, block, correction,
-    cluster, rows_tab, shift_tab,
-):
-    ka, cfg = lax.axis_index("ka"), lax.axis_index("cfg")
-    cluster_body(
-        per_moment, ka, cfg, total, configs, medium, kmap, shift_a, shift_b, square, coarse, block,
-        correction, cluster, rows_tab, shift_tab,
-    )
-
-
-def cluster_body(
-    per_moment, ka, cfg, total, configs, medium, kmap, shift_a, shift_b, square, coarse, block, correction,
-    cluster, rows_tab, shift_tab,
-):
-    tab = Tables()
-    moment_tables(configs[...].reshape(LANES, LANES), tab, rows_tab, shift_tab)
+    total_x.start(lambda to: total.at[ka])
+    configs = jnp.concatenate([first[at, 1] for at in range(n_ka)], axis=0)
+    moment_tables(configs, tab, rows_tab, shift_tab)
+    total_x.wait(lambda to: total.at[ka])
     which = iota((8, WIDE), 0)
     out = jnp.zeros((8, WIDE), F32)
+    x, x_parts, t_parts, held = [], [], [], []
     for e in range(ENERGIES):
-        y = medium_panels(medium, tab, e)
-        b_wide, c_wide = shift_panels(shift_a, shift_b, tab, e)
-        b_parts, c_parts = block_diag_c(b_wide, tab), block_diag_c(c_wide, tab)
         sum_t = (gathered_panel(total, e * 8), gathered_panel(total, e * 8 + 4))
-        x = coarse_panel(y, sum_t, tab, per_moment)
-        x_parts = block_diag_c(x, tab)
-        real, imag = cluster_matrix(x, tab)
+        x.append(coarse_panel(y[e], y_parts[e], sum_t, tab, per_moment))
+        real, imag = cluster_matrix(x[e], tab)
         cluster[e, 0] = real
         cluster[e, 1] = imag
-        t_parts = split(real), split(imag)
-        held = (cluster.at[e, 0], cluster.at[e, 1])
-        avg = rows_stage(held, t_parts, b_parts, c_parts, rows_tab, cfg * 2, ka)
+        t_parts.append((split(real), split(imag)))
+        held.append((cluster.at[e, 0], cluster.at[e, 1]))
+        avg = rows_stage(held[e], t_parts[e], b_parts[e], c_parts[e], rows_tab, cfg * 2, ka)
         for c in range(2):
             for site in range(2):
                 at = e * 4 + c * 2 + site
                 out = jnp.where(which == at, avg[c][site * 8 : site * 8 + 8], out)
+    block[...] = out
+    slot_x.start(lambda to: block)
+    slots[ka] = out
+    for e in range(ENERGIES):
+        x_parts = block_diag_c(x[e], tab)
         d = moment_stage(
-            held, t_parts, x, x_parts, b_wide, c_wide, b_parts, c_parts, shift_tab, tab
+            held[e], t_parts[e], x[e], x_parts, wide[e][0], wide[e][1], b_parts[e], c_parts[e],
+            shift_tab, tab,
         )
         re, im = correction_stage(d, square, e, kmap, tab)
         correction[e, 0:1, :] = re
         correction[e, 1:2, :] = im
         for c in range(2):
+
             def store(value, e=e, c=c):
                 coarse[e, c] = value
 
-            coarse_out(x[c], tab, store)
-    block[...] = out
-
-
-def gather_kernel(n_ka, block, average, slots, send, recv):
-    ka, cfg = lax.axis_index("ka"), lax.axis_index("cfg")
-    barrier = pltpu.get_barrier_semaphore()
-    for d in range(1, n_ka):
-        pl.semaphore_signal(barrier, inc=1, device_id=(lax.rem(ka + d, n_ka), cfg), device_id_type=MESH)
-    pl.semaphore_wait(barrier, n_ka - 1)
-
-    def copy(at, d):
-        return pltpu.make_async_remote_copy(
-            src_ref=block, dst_ref=slots.at[at], send_sem=send.at[d], recv_sem=recv.at[at],
-            device_id=(lax.rem(ka + d, n_ka), cfg), device_id_type=MESH,
-        )
-
-    for d in range(1, n_ka):
-        copy(ka, d).start()
-    slots[ka] = block[...]
-    for d in range(1, n_ka):
-        copy(lax.rem(ka + d, n_ka), d).wait_recv()
+            coarse_out(x[e][c], tab, store)
+    slot_x.wait(lambda to: block)
     for at in range(n_ka):
         for e in range(ENERGIES):
             for c in range(2):
                 for site in range(2):
                     line = e * 4 + c * 2 + site
-                    row = site * CHANS + at
-                    average[e, c, row : row + 1, :] = slots[at, line : line + 1, :]
-    for d in range(1, n_ka):
-        copy(ka, d).wait_send()
+                    to = site * CHANS + at
+                    average[e, c, to : to + 1, :] = slots[at, line : line + 1, :]
+    rows_x.drain(lambda to: row)
+    first_x.drain(lambda to: outgoing.at[to])
+    part_x.drain(lambda to: part.at[cfg])
+    total_x.drain(lambda to: total.at[ka])
+    slot_x.drain(lambda to: block)
 
 
 def shape(*dims):
@@ -619,58 +605,42 @@
     per_moment = kmap.shape[0] * n_ka * n_cfg // MOMS
     kmap = kmap.reshape(1, LANES)
     kdims = (ENERGIES, 2, CHANS, CHANS, LANES)
-    params = functools.partial(pltpu.CompilerParams, vmem_limit_bytes=48 * 1024 * 1024)
-    sums, row, square = pl.pallas_call(
-        kpoint_kernel,
-        out_shape=(shape(16, 8, LANES), shape(8, LANES), shape(*kdims)),
-        in_specs=[VMEM_SPEC] * 4 + [SMEM_SPEC],
+    dma = pltpu.SemaphoreType.DMA
+
+    def vmem(*dims):
+        return pltpu.VMEM(dims, F32)
+
+    hbm_spec = pl.BlockSpec(memory_space=pltpu.HBM)
+    return pl.pallas_call(
+        functools.partial(kernel, per_moment, n_ka, n_cfg),
+        out_shape=(
+            shape(ENERGIES, 2, CHANS, CHANS, MOMS),
+            shape(ENERGIES, 2, 2 * CHANS, WIDE),
+            shape(ENERGIES, 2, LANES),
+        ),
+        in_specs=[hbm_spec] * 2 + [VMEM_SPEC] * 2 + [SMEM_SPEC] + [VMEM_SPEC] * 2,
         out_specs=(VMEM_SPEC,) * 3,
-        scratch_shapes=[pltpu.VMEM(kdims, F32)] * 3,
-        compiler_params=params(),
-    )(structure, medium_t, kmap, occupation, cfg_weight)
-    dma = pltpu.SemaphoreType.DMA
-    total, configs = pl.pallas_call(
-        functools.partial(reduce_kernel, n_ka, n_cfg),
-        out_shape=(shape(16, 8, LANES), shape(16, 8, LANES)),
-        in_specs=[VMEM_SPEC] * 2,
-        out_specs=(VMEM_SPEC,) * 2,
         scratch_shapes=[
-            pltpu.VMEM((n_ka, 2, 8, LANES), F32),
-            pltpu.VMEM((n_ka, 2, 8, LANES), F32),
-            pltpu.VMEM((n_cfg, 8, LANES), F32),
-            pltpu.VMEM((n_cfg, 8, LANES), F32),
+            vmem(*kdims), vmem(ENERGIES, 2, CHANS, CHANS, MOMS),
+            vmem(*kdims), vmem(*kdims), vmem(*kdims), vmem(*kdims),
+            vmem(ENERGIES, 2, WIDE, WIDE),
+            vmem(SITES + 1, ALPHA, WIDE + LANES),
+            vmem(2, WIDE, WIDE),
+            vmem(8, LANES), vmem(n_cfg, 8, LANES),
+            vmem(n_ka, 2, 8, LANES), vmem(n_ka, 2, 8, LANES),
+            vmem(n_cfg, 8, LANES), vmem(n_ka, 8, LANES),
+            vmem(8, WIDE), vmem(n_ka, 8, WIDE),
+            dma((2,)),
             dma((n_cfg,)), dma((n_cfg,)),
             dma((n_ka,)), dma((n_ka,)),
             dma((n_cfg,)), dma((n_cfg,)),
             dma((n_ka,)), dma((n_ka,)),
+            dma((n_ka,)), dma((n_ka,)),
         ],
-        compiler_params=params(collective_id=0, has_side_effects=True),
-    )(sums, row)
-    coarse, block, correction = pl.pallas_call(
-        functools.partial(cluster_kernel, per_moment),
-        out_shape=(
-            shape(ENERGIES, 2, CHANS, CHANS, MOMS),
-            shape(8, WIDE),
-            shape(ENERGIES, 2, LANES),
+        compiler_params=pltpu.CompilerParams(
+            collective_id=0, has_side_effects=True, vmem_limit_bytes=48 * 1024 * 1024
         ),
-        in_specs=[VMEM_SPEC] * 7,
-        out_specs=(VMEM_SPEC,) * 3,
-        scratch_shapes=[
-            pltpu.VMEM((ENERGIES, 2, WIDE, WIDE), F32),
-            pltpu.VMEM((SITES + 1, ALPHA, WIDE + LANES), F32),
-            pltpu.VMEM((2, WIDE, WIDE), F32),
-        ],
-        compiler_params=params(),
-    )(total, configs, medium_t, kmap, shift_a, shift_b, square)
-    average = pl.pallas_call(
-        functools.partial(gather_kernel, n_ka),
-        out_shape=shape(ENERGIES, 2, 2 * CHANS, WIDE),
-        in_specs=[VMEM_SPEC],
-        out_specs=VMEM_SPEC,
-        scratch_shapes=[pltpu.VMEM((n_ka, 8, WIDE), F32), dma((n_ka,)), dma((n_ka,))],
-        compiler_params=params(collective_id=1, has_side_effects=True),
-    )(block)
-    return coarse, average, correction
+    )(structure, medium_t, kmap, occupation, cfg_weight, shift_a, shift_b)
 
 
 def solution(mesh):

time: 62.9 us -> 46.7 us (0.74); the launches traced: 61.7 us -> 46.4 us
  Pallas kernels: 56.9 us -> 38.8 us
  local copies, waits for them, and re-layouts: 3.41 us -> 6.28 us
    pallas_call x4 -> x1, Pallas kernels: 56.9 us -> 38.8 us  [per_device(): pl.pallas_call(functools.partial(kernel, per_moment, n_ka, n_cfg), out_sh...]
    unnamed x15, local copies, waits for them, and re-layouts: 3.41 us -> 6.28 us
where the time goes in v2:
time: 46.7 us; the launch traced here: 46.4 us
  Pallas kernels  38.8 us (83%)
  local copies, waits for them, and re-layouts  6.28 us (13%)
  between operations  1.31 us (3%)
    pallas_call x1, Pallas kernels, per_device(): pl.pallas_call(functools.partial(kernel, per_moment, n_ka, n_cfg), out_sh...  38.8 us
    unnamed x15, local copies, waits for them, and re-layouts  6.28 us

profile of v2, /device:TPU:1, one launch (start us, length us, event | category | flops | bytes accessed | tf_op | source)
XLA Modules:
  0.0 46.4 jit_solution(10239046244898609694)
XLA Ops:
  1.3 0.0 copy-start.4
  1.3 0.0 copy-start.5
  1.3 0.6 %copy-done.4 = s32[128]{0:T(128)S(1)} copy-done((s32[128]{0:T(128)S(1)}, s32[128]{0:T(128)}, u32[]{:S(2)}) %copy-start.4) | copy-done | bytes 536
  1.9 0.0 copy-done.5
  2.0 0.0 copy-start
  2.0 1.0 %copy-done = f32[2,2,16,16,128]{4,3,2,1,0:T(8,128)S(1)} copy-done((f32[2,2,16,16,128]{4,3,2,1,0:T(8,128)S(1)}, f32[2,2,16,16,128]{4,3,2,1,0:T(8,128)}, u32[]{:S(2)}) %copy-start) | copy-done | bytes 524312
  3.0 0.0 copy-start.1
  3.0 1.0 %copy-done.1 = f32[2,2,16,16,16]{4,3,2,1,0:T(8,128)S(1)} copy-done((f32[2,2,16,16,16]{4,3,2,1,0:T(8,128)S(1)}, f32[2,2,16,16,16]{4,3,2,1,0:T(8,128)}, u32[]{:S(2)}) %copy-start.1) | copy-done | bytes 65560
  4.0 0.0 copy-start.2
  4.0 0.8 %copy-done.2 = f32[2,2,16,16]{3,2,1,0:T(8,128)S(1)} copy-done((f32[2,2,16,16]{3,2,1,0:T(8,128)S(1)}, f32[2,2,16,16]{3,2,1,0:T(8,128)}, u32[]{:S(2)}) %copy-start.2) | copy-done | bytes 4120
  4.8 0.0 copy-start.3
  4.8 0.8 %copy-done.3 = f32[2,2,16,16]{3,2,1,0:T(8,128)S(1)} copy-done((f32[2,2,16,16]{3,2,1,0:T(8,128)S(1)}, f32[2,2,16,16]{3,2,1,0:T(8,128)}, u32[]{:S(2)}) %copy-start.3) | copy-done | bytes 4120
  5.6 38.8 %shard_map.94 = (f32[2,2,16,16,16]{4,3,2,1,0:T(8,128)S(1)}, f32[2,2,32,256]{3,2,1,0:T(8,128)S(1)}, f32[2,2,128]{2,1,0:T(2,128)S(1)}) custom-call(f32[2,2,16,16,128]{4,3,2,1,0:T(8,128)S(1)} %copy-done, f32[2,2,16,16,16]{4,3,2,1,0:T(8,128)S(1)} %copy-done.1, s32[1,128]{1,0:T(1,128)S(1)} %bitcast.1, s32[1,16]{1,0:T(1,128)S(1)} %copy-done.5, f32[1]{0:T(128)S(6)} %copy.13.weight, ...), custom_call_target="tpu_custom_call" | custom-call | tf_op jit(solution)/shard_map/pallas_call | solution.py:614
  44.3 0.8 %copy.14 = f32[2,2,16,16,16]{4,3,2,1,0:T(8,128)} copy(f32[2,2,16,16,16]{4,3,2,1,0:T(8,128)S(1)} %get-tuple-element.6) | data formatting | bytes 131072
  45.1 0.7 %copy.15 = f32[2,2,32,256]{3,2,1,0:T(8,128)} copy(f32[2,2,32,256]{3,2,1,0:T(8,128)S(1)} %get-tuple-element.7) | data formatting | bytes 262144
  45.8 0.6 %copy.16 = f32[2,2,128]{2,1,0:T(2,128)} copy(f32[2,2,128]{2,1,0:T(2,128)S(1)} %get-tuple-element.8) | data formatting | bytes 4096
Async XLA Ops:
  1.3 0.7 %copy-start.4 = (s32[128]{0:T(128)S(1)}, s32[128]{0:T(128)}, u32[]{:S(2)}) copy-start(s32[128]{0:T(128)} %param.9) | copy-start | bytes 1540
  1.3 0.7 %copy-start.5 = (s32[1,16]{1,0:T(1,128)S(1)}, s32[1,16]{1,0:T(1,128)}, u32[]{:S(2)}) copy-start(s32[1,16]{1,0:T(1,128)} %occupation.1) | copy-start | bytes 196
  2.0 1.0 %copy-start = (f32[2,2,16,16,128]{4,3,2,1,0:T(8,128)S(1)}, f32[2,2,16,16,128]{4,3,2,1,0:T(8,128)}, u32[]{:S(2)}) copy-start(f32[2,2,16,16,128]{4,3,2,1,0:T(8,128)} %structure_hbm.1) | copy-start | bytes 1572868
  3.0 1.0 %copy-start.1 = (f32[2,2,16,16,16]{4,3,2,1,0:T(8,128)S(1)}, f32[2,2,16,16,16]{4,3,2,1,0:T(8,128)}, u32[]{:S(2)}) copy-start(f32[2,2,16,16,16]{4,3,2,1,0:T(8,128)} %medium_hbm.1) | copy-start | bytes 196612
  4.0 0.8 %copy-start.2 = (f32[2,2,16,16]{3,2,1,0:T(8,128)S(1)}, f32[2,2,16,16]{3,2,1,0:T(8,128)}, u32[]{:S(2)}) copy-start(f32[2,2,16,16]{3,2,1,0:T(8,128)} %shift_a.1) | copy-start | bytes 12292
  4.8 0.8 %copy-start.3 = (f32[2,2,16,16]{3,2,1,0:T(8,128)S(1)}, f32[2,2,16,16]{3,2,1,0:T(8,128)}, u32[]{:S(2)}) copy-start(f32[2,2,16,16]{3,2,1,0:T(8,128)} %shift_b.1) | copy-start | bytes 12292

commit v3 on v2

--- a/solution.py
+++ b/solution.py
@@ -33,12 +33,16 @@
 
 def dot_exact(x, right, dims=NN):
     high, low = split(x)
-    return dot(high, right, dims) + dot(low, right, dims)
+    rows = x.shape[0]
+    both = dot(jnp.concatenate([high, low], axis=0), right, dims)
+    return both[:rows] + both[rows:]
 
 
 def dot3(x, right, dims=NN):
     high, low = split(x)
-    return dot(high, right[0], dims) + (dot(low, right[0], dims) + dot(high, right[1], dims))
+    rows = x.shape[0]
+    both = dot(jnp.concatenate([high, low], axis=0), right[0], dims)
+    return both[:rows] + (both[rows:] + dot(high, right[1], dims))
 
 
 def cdot(x, right, dims=NN):
@@ -149,14 +153,16 @@
 
 def kpoint_sums(inner, kmap, write_tile):
     rows, lanes = iota((WIDE, LANES), 0), kmap[...]
-    onehot_t = ((rows >> 4) == lanes).astype(F32).astype(BF16)
+    onehot = jnp.transpose(((rows >> 4) == lanes).astype(F32)).astype(BF16)
+    onehot = jnp.concatenate([onehot, onehot], axis=0)
     row_block = iota((WIDE, WIDE), 0) >> 4
     col_in = iota((WIDE, WIDE), 1) & 15
     keep = row_block == col_in
     for e in range(ENERGIES):
         for c in range(2):
             flat = inner[e, c].reshape(WIDE, LANES)
-            by_mom = jnp.where(keep, dot_exact(flat, onehot_t, NT), 0.0)
+            parts = jnp.concatenate(split(flat), axis=1)
+            by_mom = jnp.where(keep, dot(parts, onehot), 0.0)
             panel = jnp.sum(by_mom.reshape(CHANS, CHANS, WIDE), axis=0)
             for half in range(2):
                 for side in range(2):
@@ -166,25 +172,24 @@
                     )
 
 
-def kpoint_squares(spread, factor, tau, square):
-    for e in range(ENERGIES):
-        y, f, t, s = spread.at[e], factor.at[e], tau.at[e], square.at[e]
-
-        def put_q(a, re, im, s=s, f=f):
-            s[0, a] = f[0, a] + re
-            s[1, a] = f[1, a] + im
-
-        def put_t(a, re, im, t=t, y=y):
-            t[0, a] = y[0, a] + re
-            t[1, a] = y[1, a] + im
-
-        def put_s(a, re, im, s=s):
-            s[0, a] = re
-            s[1, a] = im
-
-        kpoint_mul(put_q, f, f)
-        kpoint_mul(put_t, s, y)
-        kpoint_mul(put_s, t, t)
+def kpoint_squares(spread, factor, tau, square, e):
+    y, f, t, s = spread.at[e], factor.at[e], tau.at[e], square.at[e]
+
+    def put_q(a, re, im):
+        s[0, a] = f[0, a] + re
+        s[1, a] = f[1, a] + im
+
+    def put_t(a, re, im):
+        t[0, a] = y[0, a] + re
+        t[1, a] = y[1, a] + im
+
+    def put_s(a, re, im):
+        s[0, a] = re
+        s[1, a] = im
+
+    kpoint_mul(put_q, f, f)
+    kpoint_mul(put_t, s, y)
+    kpoint_mul(put_s, t, t)
 
 
 def config_row(occupation, weight, row):
@@ -251,34 +256,87 @@
     return b, c
 
 
-def coarse_panel(y, y_parts, sum_t, tab, per_moment):
+def coarse_panels(y, y_b, y_c, y_all, sum_t, tab, per_moment):
     left = cdot(y, block_diag_c(sum_t, tab), NT)
-    both = cdot(left, y_parts)
     scale = 1.0 / per_moment
-    return y[0] + scale * both[0], y[1] + scale * both[1]
-
-
-def cluster_matrix(x, tab):
-    re, im = tile_rows(x[0], SITES), tile_rows(x[1], SITES)
-    scale = 1.0 / SITES
-    left_r = (re * tab.cos - im * tab.sin) * scale
-    left_i = (re * tab.sin + im * tab.cos) * scale
-    real = dot_exact(left_r, tab.wave_cos, NT) + dot_exact(left_i, tab.wave_sin, NT)
-    imag = dot_exact(left_i, tab.wave_cos, NT) - dot_exact(left_r, tab.wave_sin, NT)
-    return real, imag
-
-
-def rows_stage(cluster, t_parts, b_parts, c_parts, rows_tab, site0, chan):
-    def own(ref):
-        first = ref[pl.ds(site0 * CHANS + chan, 1), :]
-        second = ref[pl.ds((site0 + 1) * CHANS + chan, 1), :]
-        return jnp.concatenate(
-            [jnp.broadcast_to(first, (8, WIDE)), jnp.broadcast_to(second, (8, WIDE))], axis=0
+    left = (left[0] * scale, left[1] * scale)
+    out = []
+    for base, parts in zip((y, y_b, y_c), y_all):
+        step = cdot(left, parts)
+        out.append((base[0] + step[0], base[1] + step[1]))
+    return out
+
+
+def first_rows(panels, lines, tab, site0):
+    mom = iota((16, WIDE), 1) >> 4
+    second = (iota((16, WIDE), 0) >> 3).astype(jnp.int32)
+    cos, sin = cos_sin(quarter_turns(mom, site0 + second))
+    left_r, left_i = [], []
+    for panel, line in zip(panels, lines):
+        lr, li = jnp.broadcast_to(line[0], (16, WIDE)), jnp.broadcast_to(line[1], (16, WIDE))
+        left_r += [panel[0], lr * cos - li * sin]
+        left_i += [panel[1], lr * sin + li * cos]
+    rows = 32 * len(panels)
+    both = jnp.concatenate(left_r + left_i, axis=0) * (1.0 / SITES)
+    by_cos = dot_exact(both, tab.wave_cos, NT)
+    by_sin = dot_exact(both, tab.wave_sin, NT)
+    real = by_cos[:rows] + by_sin[rows:]
+    imag = by_cos[rows:] - by_sin[:rows]
+    out = []
+    for at in range(0, rows, 32):
+        out.append(
+            (
+                (real[at : at + 16], imag[at : at + 16]),
+                (real[at + 16 : at + 32], imag[at + 16 : at + 32]),
+            )
         )
-
-    start = (own(cluster[0]), own(cluster[1]))
-    with_b = cdot(start, b_parts)
-    with_c = cdot(start, c_parts)
+    return out
+
+
+def swap_blocks(x, bit):
+    step = 16 * bit
+    up = pltpu.roll(x, LANES - step, axis=1)
+    if bit == 4:
+        return up
+    down = pltpu.roll(x, step, axis=1)
+    high = ((iota(x.shape, 1) >> 4) & bit) != 0
+    return jnp.where(high, down, up)
+
+
+def all_swaps(x):
+    out = {0: x}
+    out[4] = swap_blocks(x, 4)
+    for at in (0, 4):
+        out[at | 2] = swap_blocks(out[at], 2)
+    for at in (0, 2, 4, 6):
+        out[at | 1] = swap_blocks(out[at], 1)
+    return out
+
+
+def translated(panel):
+    low = all_swaps(panel[:, 0:LANES])
+    top = all_swaps(panel[:, LANES:WIDE])
+
+    def whole(a, b):
+        rows = [jnp.concatenate([a[q], b[q]], axis=1) for q in range(8)]
+        rows += [jnp.concatenate([b[q ^ 7], a[q]], axis=1) for q in range(8)]
+        return jnp.concatenate(rows, axis=0)
+
+    low_parts = {q: split(v) for q, v in low.items()}
+    top_parts = {q: split(v) for q, v in top.items()}
+    parts = tuple(
+        whole({q: v[p] for q, v in low_parts.items()}, {q: v[p] for q, v in top_parts.items()})
+        for p in range(2)
+    )
+    return whole(low, top), parts
+
+
+def translated_c(panel):
+    real, imag = translated(panel[0]), translated(panel[1])
+    return (real[0], imag[0]), (real[1], imag[1])
+
+
+def rows_stage(start, with_b, with_c, t_parts, tb_parts, tc_parts, rows_tab):
     row = iota((ALPHA, WIDE), 0)
     block = iota((ALPHA, WIDE), 1) >> 4
 
@@ -290,57 +348,44 @@
             out.append(jnp.where(row == block, uc, jnp.where(row == SITES, ub, 0.0)))
         return jnp.concatenate(out, axis=0)
 
-    hop = cdot((opened(0), opened(1)), t_parts)
-    plain, dressed = [[], []], [[], []]
+    begin = (opened(0), opened(1))
+    hop_b = cdot(begin, tb_parts)
+    hop_c = cdot(begin, tc_parts)
+    inner = []
     for c in range(2):
+        out = []
         for site in range(2):
-            f = jnp.zeros((ALPHA, WIDE), F32)
-            h = jnp.zeros((ALPHA, WIDE), F32)
+            g = jnp.zeros((ALPHA, WIDE), F32)
             for s in range(SITES + 1):
-                line = hop[c][site * ALPHA + s : site * ALPHA + s + 1]
+                at = site * ALPHA + s
                 pair = rows_tab[s, :, WIDE : WIDE + LANES]
-                f = f + jnp.concatenate([pair, pair], axis=1) * line
-                h = h + rows_tab[s, :, 0:WIDE] * line
-            plain[c].append(f)
-            dressed[c].append(h)
-    plain = tuple(jnp.concatenate(p, axis=0) for p in plain)
-    dressed = tuple(jnp.concatenate(d, axis=0) for d in dressed)
-    by_b = cdot(plain, b_parts)
-    by_c = cdot(dressed, c_parts)
-    inner = (by_b[0] + by_c[0], by_b[1] + by_c[1])
-    second = cdot(inner, t_parts)
+                g = g + jnp.concatenate([pair, pair], axis=1) * hop_b[c][at : at + 1]
+                g = g + rows_tab[s, :, 0:WIDE] * hop_c[c][at : at + 1]
+            out.append(g)
+        inner.append(jnp.concatenate(out, axis=0))
     mean = rows_tab[SITES, SITES : SITES + 1, 0:WIDE]
 
     def eight(parts):
         return jnp.concatenate([jnp.broadcast_to(p, (8, WIDE)) for p in parts], axis=0)
 
-    for_b, for_c, rest = [], [], []
+    ends = tuple(
+        eight([inner[c][site * ALPHA + SITES : site * ALPHA + SITES + 1] for site in range(2)])
+        for c in range(2)
+    )
+    by_b = cdot(ends, tb_parts)
+    by_c = cdot(tuple(inner), tc_parts)
+    z = []
     for c in range(2):
-        last_b, last_c, known = [], [], []
+        picked = []
         for site in range(2):
-            lines = second[c][site * ALPHA : site * ALPHA + ALPHA]
-            picked = jnp.sum(jnp.where(row == block, lines, 0.0), axis=0, keepdims=True)
-            last_b.append(lines[SITES : SITES + 1])
-            last_c.append(picked)
-            known.append(
-                with_b[c][site * 8 : site * 8 + 1]
-                + with_c[c][site * 8 : site * 8 + 1] * mean
-                - inner[c][site * ALPHA + SITES : site * ALPHA + SITES + 1]
-            )
-        for_b.append(eight(last_b))
-        for_c.append(eight(last_c))
-        rest.append(eight(known))
-    by_b = cdot(tuple(for_b), b_parts)
-    by_c = cdot(tuple(for_c), c_parts)
-    z = (rest[0] + by_b[0] + by_c[0], rest[1] + by_b[1] + by_c[1])
-    last = cdot(z, t_parts)
+            lines = by_c[c][site * ALPHA : site * ALPHA + ALPHA]
+            picked.append(jnp.sum(jnp.where(row == block, lines, 0.0), axis=0, keepdims=True))
+        z.append(with_b[c] + with_c[c] * mean - ends[c] + by_b[c] + eight(picked))
+    last = cdot(tuple(z), t_parts)
     return start[0] - last[0], start[1] - last[1]
 
 
-def moment_stage(cluster, t_parts, x, x_parts, b_wide, c_wide, b_parts, c_parts, shift_tab, tab):
-    top = (cluster[0][0:CHANS, :], cluster[1][0:CHANS, :])
-    top_parts = csplit(top)
-
+def moment_stage(top_b, top_c, tc_full, tb_parts, tc_parts, x, x_parts, b_wide, c_wide, shift_tab, tab):
     def head(wide):
         return wide[0][:, 0:CHANS], wide[1][:, 0:CHANS]
 
@@ -349,48 +394,29 @@
         jnp.concatenate([b_in[0], c_in[0]], axis=0),
         jnp.concatenate([b_in[1], c_in[1]], axis=0),
     )
-    lead = cdot(small, top_parts)
-    lead_b = (lead[0][0:CHANS], lead[1][0:CHANS])
-    lead_c = (lead[0][CHANS:], lead[1][CHANS:])
-    then_b = cdot(lead, b_parts)
-    then_c = cdot(lead, c_parts)
+    lead_b = cdot(small, csplit(top_b))
+    lead_c = cdot(small, csplit(top_c))
+    bb, cb = [v[0:CHANS] for v in lead_b], [v[CHANS:] for v in lead_b]
+    bc, cc = [v[0:CHANS] for v in lead_c], [v[CHANS:] for v in lead_c]
     two = shift_tab[1, 0:1, :]
     mean = shift_tab[1, 0:1, 0:1]
-
-    def mix(c):
-        bb, cb = then_b[c][0:CHANS], then_b[c][CHANS:]
-        bc, cc = then_c[c][0:CHANS], then_c[c][CHANS:]
-        return bb + mean * (bc + cb) + two * cc, bb, cb
-
-    re, im = mix(0), mix(1)
-    hop = cdot((jnp.concatenate(re, axis=0), jnp.concatenate(im, axis=0)), t_parts)
+    zero = [bb[c] + mean * (bc[c] + cb[c]) + two * cc[c] for c in range(2)]
+    by_b = cdot(tuple(zero), tb_parts)
+    by_c = cdot(tuple(jnp.concatenate([bb[c], cb[c]], axis=0) for c in range(2)), tc_parts)
 
     def scaled(which):
-        return (
-            split(cluster[0][...] * shift_tab[which]),
-            split(cluster[1][...] * shift_tab[which]),
-        )
-
-    pair = cdot((then_c[0][0:CHANS], then_c[1][0:CHANS]), scaled(0))
-    triple = cdot((then_c[0][CHANS:], then_c[1][CHANS:]), scaled(1))
-    for_b, for_c = [], []
+        return split(tc_full[0] * shift_tab[which]), split(tc_full[1] * shift_tab[which])
+
+    pair = cdot(tuple(bc), scaled(0))
+    triple = cdot(tuple(cc), scaled(1))
+    line = []
     for c in range(2):
-        h = hop[c]
-        for_b.append(h[0:CHANS] - (lead_b[c] + mean * lead_c[c]))
-        for_c.append(
-            mean * h[CHANS : 2 * CHANS]
-            + two * h[2 * CHANS : 3 * CHANS]
-            + pair[c]
-            + triple[c]
-            - (mean * lead_b[c] + two * lead_c[c])
-        )
-    by_b = cdot(tuple(for_b), b_parts)
-    by_c = cdot(tuple(for_c), c_parts)
-    line_r, line_i = by_b[0] + by_c[0], by_b[1] + by_c[1]
-    m_r = dot_exact(line_r, tab.wave_cos) - dot_exact(line_i, tab.wave_sin)
-    m_i = dot_exact(line_r, tab.wave_sin) + dot_exact(line_i, tab.wave_cos)
-    m_r = m_r + b_wide[0] + mean * c_wide[0]
-    m_i = m_i + b_wide[1] + mean * c_wide[1]
+        third = by_b[c] + mean * by_c[c][0:CHANS] + two * by_c[c][CHANS:] + pair[c] + triple[c]
+        line.append(third - (bb[c] + mean * (cb[c] + bc[c]) + two * cc[c]))
+    m_cos = dot_exact(jnp.concatenate(line, axis=0), tab.wave_cos)
+    m_sin = dot_exact(jnp.concatenate(line, axis=0), tab.wave_sin)
+    m_r = m_cos[:CHANS] - m_sin[CHANS:] + b_wide[0] + mean * c_wide[0]
+    m_i = m_sin[:CHANS] + m_cos[CHANS:] + b_wide[1] + mean * c_wide[1]
     d = cdot(cdot(x, block_diag_c((m_r, m_i), tab)), x_parts)
     return -d[0], -d[1]
 
@@ -432,8 +458,8 @@
 
 
 def gathered_panel(tiles, at):
-    top = jnp.concatenate([tiles[at], tiles[at + 1]], axis=1)
-    low = jnp.concatenate([tiles[at + 2], tiles[at + 3]], axis=1)
+    top = jnp.concatenate([tiles[at // 2, 0], tiles[at // 2, 1]], axis=1)
+    low = jnp.concatenate([tiles[at // 2 + 1, 0], tiles[at // 2 + 1, 1]], axis=1)
     return jnp.concatenate([top, low], axis=0)
 
 
@@ -478,95 +504,116 @@
 
 def kernel(
     per_moment, n_ka, n_cfg,
-    structure_hbm, medium_hbm, kmap, occupation, weight, shift_a, shift_b,
+    structure_hbm, medium_hbm, kmap_hbm, occupation_hbm, weight, shift_a_hbm, shift_b_hbm,
     coarse, average, correction,
-    structure, medium, spread, factor, inner, square, cluster, rows_tab, shift_tab,
+    structure, medium, kmap, occupation, shift_a, shift_b,
+    spread, factor, inner, square, panels, rows_tab, shift_tab,
     row, own_rows, outgoing, first, part, total, block, slots,
     load_sem, row_send, row_recv, first_send, first_recv, part_send, part_recv,
     total_send, total_recv, slot_send, slot_recv,
 ):
-    barrier = greet(n_ka, n_cfg)
+    pairs = (
+        (medium_hbm, medium), (kmap_hbm, kmap), (structure_hbm, structure),
+        (occupation_hbm, occupation), (shift_a_hbm, shift_a), (shift_b_hbm, shift_b),
+    )
     loads = [
-        pltpu.make_async_copy(medium_hbm, medium, load_sem.at[0]),
-        pltpu.make_async_copy(structure_hbm, structure, load_sem.at[1]),
+        pltpu.make_async_copy(source, to, load_sem.at[at]) for at, (source, to) in enumerate(pairs)
     ]
     for load in loads:
         load.start()
+    barrier = greet(n_ka, n_cfg)
     rows_x = Exchange("cfg", n_cfg, own_rows, row_send, row_recv)
-    first_x = Exchange("ka", n_ka, first, first_send, first_recv)
-    part_x = Exchange("cfg", n_cfg, part, part_send, part_recv)
-    total_x = Exchange("ka", n_ka, total, total_send, total_recv)
+    first_x = Exchange("cfg", n_cfg, first, first_send, first_recv)
+    part_x = Exchange("ka", n_ka, part, part_send, part_recv)
+    total_x = Exchange("cfg", n_cfg, total, total_send, total_recv)
     slot_x = Exchange("ka", n_ka, slots, slot_send, slot_recv)
-    ka, cfg = first_x.me, rows_x.me
+    ka, cfg = part_x.me, rows_x.me
+    loads[0].wait()
+    loads[1].wait()
+    spread_medium(medium, kmap, spread)
+    loads[2].wait()
+    kpoint_inner(structure, spread, factor, inner, 0)
+    for load in loads[3:]:
+        load.wait()
     config_row(occupation, weight, row)
-    loads[0].wait()
-    spread_medium(medium, kmap, spread)
-    loads[1].wait()
-    kpoint_inner(structure, spread, factor, inner, 0)
     pl.semaphore_wait(barrier, n_ka + n_cfg - 2)
     rows_x.start(lambda to: row)
     own_rows[cfg] = row[...]
     kpoint_inner(structure, spread, factor, inner, 1)
 
     def write(at, value):
-        outgoing[at, 0] = value
+        outgoing[at // 2, at % 2] = value
 
     kpoint_sums(inner, kmap, write)
+    first_x.start(lambda to: outgoing.at[to])
+    first[cfg] = outgoing[cfg]
+    kpoint_squares(spread, factor, inner, square, 0)
     rows_x.wait(lambda to: row)
     line = iota((8, LANES), 0)
     group = jnp.zeros((8, LANES), F32)
     for at in range(n_cfg):
         group = group + jnp.where(line == at, own_rows[at], 0.0)
-    for at in range(n_ka):
-        outgoing[at, 1] = group
-    first_x.start(lambda to: outgoing.at[to])
-    first[ka] = outgoing[ka]
-    kpoint_squares(spread, factor, inner, square)
     first_x.wait(lambda to: outgoing.at[to])
-    value = first[0, 0]
+    value = [first[0, 0], first[0, 1]]
+    for at in range(1, n_cfg):
+        value = [value[0] + first[at, 0], value[1] + first[at, 1]]
+    part[ka, 0] = value[0]
+    part[ka, 1] = value[1]
+    part[ka, 2] = group
+    part_x.start(lambda to: part.at[ka])
+    kpoint_squares(spread, factor, inner, square, 1)
+    tab = Tables()
+    energies = range(ENERGIES)
+    y = [medium_panels(medium, tab, e) for e in energies]
+    wide = [shift_panels(shift_a, shift_b, tab, e) for e in energies]
+    y_b = [cdot(y[e], block_diag_c(wide[e][0], tab)) for e in energies]
+    y_c = [cdot(y[e], block_diag_c(wide[e][1], tab)) for e in energies]
+    y_all = [
+        (block_diag_c(y[e], tab), block_diag_c(y_b[e], tab), block_diag_c(y_c[e], tab))
+        for e in energies
+    ]
+    part_x.wait(lambda to: part.at[ka])
+    value = [part[0, 0], part[0, 1]]
     for at in range(1, n_ka):
-        value = value + first[at, 0]
-    part[cfg] = value
-    part_x.start(lambda to: part.at[cfg])
-    tab = Tables()
-    y = [medium_panels(medium, tab, e) for e in range(ENERGIES)]
-    y_parts = [block_diag_c(y[e], tab) for e in range(ENERGIES)]
-    wide = [shift_panels(shift_a, shift_b, tab, e) for e in range(ENERGIES)]
-    b_parts = [block_diag_c(wide[e][0], tab) for e in range(ENERGIES)]
-    c_parts = [block_diag_c(wide[e][1], tab) for e in range(ENERGIES)]
-    part_x.wait(lambda to: part.at[cfg])
-    value = part[0]
-    for at in range(1, n_cfg):
-        value = value + part[at]
-    total[ka] = value
-    total_x.start(lambda to: total.at[ka])
-    configs = jnp.concatenate([first[at, 1] for at in range(n_ka)], axis=0)
+        value = [value[0] + part[at, 0], value[1] + part[at, 1]]
+    total[cfg, 0] = value[0]
+    total[cfg, 1] = value[1]
+    total_x.start(lambda to: total.at[cfg])
+    configs = jnp.concatenate([part[at, 2] for at in range(n_ka)], axis=0)
     moment_tables(configs, tab, rows_tab, shift_tab)
-    total_x.wait(lambda to: total.at[ka])
+    total_x.wait(lambda to: total.at[cfg])
     which = iota((8, WIDE), 0)
     out = jnp.zeros((8, WIDE), F32)
-    x, x_parts, t_parts, held = [], [], [], []
-    for e in range(ENERGIES):
+    kept = []
+    for e in energies:
         sum_t = (gathered_panel(total, e * 8), gathered_panel(total, e * 8 + 4))
-        x.append(coarse_panel(y[e], y_parts[e], sum_t, tab, per_moment))
-        real, imag = cluster_matrix(x[e], tab)
-        cluster[e, 0] = real
-        cluster[e, 1] = imag
-        t_parts.append((split(real), split(imag)))
-        held.append((cluster.at[e, 0], cluster.at[e, 1]))
-        avg = rows_stage(held[e], t_parts[e], b_parts[e], c_parts[e], rows_tab, cfg * 2, ka)
+        x, x_b, x_c = coarse_panels(y[e], y_b[e], y_c[e], y_all[e], sum_t, tab, per_moment)
+        lines = []
+        for at, panel in enumerate((x, x_b, x_c)):
+            panels[e, at, 0] = panel[0]
+            panels[e, at, 1] = panel[1]
+            lines.append(
+                (panels[e, at, 0, pl.ds(ka, 1), :], panels[e, at, 1, pl.ds(ka, 1), :])
+            )
+        (top, start), (top_b, with_b), (top_c, with_c) = first_rows(
+            (x, x_b, x_c), lines, tab, cfg * 2
+        )
+        t_parts = translated_c(top)[1]
+        tb_parts = translated_c(top_b)[1]
+        tc_full, tc_parts = translated_c(top_c)
+        avg = rows_stage(start, with_b, with_c, t_parts, tb_parts, tc_parts, rows_tab)
         for c in range(2):
             for site in range(2):
                 at = e * 4 + c * 2 + site
                 out = jnp.where(which == at, avg[c][site * 8 : site * 8 + 8], out)
+        kept.append((top_b, top_c, tc_full, tb_parts, tc_parts, x))
     block[...] = out
     slot_x.start(lambda to: block)
     slots[ka] = out
-    for e in range(ENERGIES):
-        x_parts = block_diag_c(x[e], tab)
+    for e in energies:
+        x = kept[e][5]
         d = moment_stage(
-            held[e], t_parts[e], x[e], x_parts, wide[e][0], wide[e][1], b_parts[e], c_parts[e],
-            shift_tab, tab,
+            *kept[e], block_diag_c(x, tab), wide[e][0], wide[e][1], shift_tab, tab
         )
         re, im = correction_stage(d, square, e, kmap, tab)
         correction[e, 0:1, :] = re
@@ -576,10 +623,10 @@
             def store(value, e=e, c=c):
                 coarse[e, c] = value
 
-            coarse_out(x[e][c], tab, store)
+            coarse_out(x[c], tab, store)
     slot_x.wait(lambda to: block)
     for at in range(n_ka):
-        for e in range(ENERGIES):
+        for e in energies:
             for c in range(2):
                 for site in range(2):
                     line = e * 4 + c * 2 + site
@@ -587,9 +634,18 @@
                     average[e, c, to : to + 1, :] = slots[at, line : line + 1, :]
     rows_x.drain(lambda to: row)
     first_x.drain(lambda to: outgoing.at[to])
-    part_x.drain(lambda to: part.at[cfg])
-    total_x.drain(lambda to: total.at[ka])
+    part_x.drain(lambda to: part.at[ka])
+    total_x.drain(lambda to: total.at[cfg])
     slot_x.drain(lambda to: block)
+
+
+def output_kernel(coarse, average, correction, coarse_out_ref, average_out, correction_out, sem):
+    pairs = ((coarse, coarse_out_ref), (average, average_out), (correction, correction_out))
+    copies = [pltpu.make_async_copy(a, b, sem.at[at]) for at, (a, b) in enumerate(pairs)]
+    for copy in copies:
+        copy.start()
+    for copy in copies:
+        copy.wait()
 
 
 def shape(*dims):
@@ -610,37 +666,47 @@
     def vmem(*dims):
         return pltpu.VMEM(dims, F32)
 
-    hbm_spec = pl.BlockSpec(memory_space=pltpu.HBM)
-    return pl.pallas_call(
+    any_spec = pl.BlockSpec(memory_space=pl.ANY)
+    shapes = (
+        shape(ENERGIES, 2, CHANS, CHANS, MOMS),
+        shape(ENERGIES, 2, 2 * CHANS, WIDE),
+        shape(ENERGIES, 2, LANES),
+    )
+    results = pl.pallas_call(
         functools.partial(kernel, per_moment, n_ka, n_cfg),
-        out_shape=(
-            shape(ENERGIES, 2, CHANS, CHANS, MOMS),
-            shape(ENERGIES, 2, 2 * CHANS, WIDE),
-            shape(ENERGIES, 2, LANES),
-        ),
-        in_specs=[hbm_spec] * 2 + [VMEM_SPEC] * 2 + [SMEM_SPEC] + [VMEM_SPEC] * 2,
+        out_shape=shapes,
+        in_specs=[any_spec] * 4 + [SMEM_SPEC] + [any_spec] * 2,
         out_specs=(VMEM_SPEC,) * 3,
         scratch_shapes=[
             vmem(*kdims), vmem(ENERGIES, 2, CHANS, CHANS, MOMS),
+            pltpu.VMEM((1, LANES), jnp.int32), pltpu.VMEM((1, SITES), jnp.int32),
+            vmem(ENERGIES, 2, CHANS, CHANS), vmem(ENERGIES, 2, CHANS, CHANS),
             vmem(*kdims), vmem(*kdims), vmem(*kdims), vmem(*kdims),
-            vmem(ENERGIES, 2, WIDE, WIDE),
+            vmem(ENERGIES, 3, 2, CHANS, WIDE),
             vmem(SITES + 1, ALPHA, WIDE + LANES),
             vmem(2, WIDE, WIDE),
             vmem(8, LANES), vmem(n_cfg, 8, LANES),
-            vmem(n_ka, 2, 8, LANES), vmem(n_ka, 2, 8, LANES),
-            vmem(n_cfg, 8, LANES), vmem(n_ka, 8, LANES),
+            vmem(n_cfg, 2, 8, LANES), vmem(n_cfg, 2, 8, LANES),
+            vmem(n_ka, 3, 8, LANES), vmem(n_cfg, 2, 8, LANES),
             vmem(8, WIDE), vmem(n_ka, 8, WIDE),
-            dma((2,)),
+            dma((6,)),
+            dma((n_cfg,)), dma((n_cfg,)),
             dma((n_cfg,)), dma((n_cfg,)),
             dma((n_ka,)), dma((n_ka,)),
             dma((n_cfg,)), dma((n_cfg,)),
             dma((n_ka,)), dma((n_ka,)),
-            dma((n_ka,)), dma((n_ka,)),
         ],
         compiler_params=pltpu.CompilerParams(
-            collective_id=0, has_side_effects=True, vmem_limit_bytes=48 * 1024 * 1024
+            collective_id=0, has_side_effects=True, vmem_limit_bytes=56 * 1024 * 1024
         ),
     )(structure, medium_t, kmap, occupation, cfg_weight, shift_a, shift_b)
+    return pl.pallas_call(
+        output_kernel,
+        out_shape=shapes,
+        in_specs=[any_spec] * 3,
+        out_specs=(any_spec,) * 3,
+        scratch_shapes=[dma((3,))],
+    )(*results)
 
 
 def solution(mesh):

time: 46.7 us -> 57.2 us (1.22)
  Pallas kernels: 38.8 us -> 55.8 us
  local copies, waits for them, and re-layouts: 6.28 us -> 0 us
    pallas_call x0 -> x1, Pallas kernels: none -> 21 us  [per_device(): pl.pallas_call(output_kernel, out_shape=shapes, in_specs=[any_spec] * 3,...]
    unnamed x15 -> x0, local copies, waits for them, and re-layouts: 6.28 us -> none
    pallas_call x1, Pallas kernels: 38.8 us -> 34.8 us  [per_device(): pl.pallas_call(functools.partial(kernel, per_moment, n_ka, n_cfg), out_sh...]
where the time goes in v3:
time: 57.2 us; the launch traced here: 57.1 us
  Pallas kernels  55.8 us (98%)
  between operations  1.29 us (2%)
    pallas_call x1, Pallas kernels, per_device(): pl.pallas_call(functools.partial(kernel, per_moment, n_ka, n_cfg), out_sh...  34.8 us
    pallas_call x1, Pallas kernels, per_device(): pl.pallas_call(output_kernel, out_shape=shapes, in_specs=[any_spec] * 3,...  21 us

profile of v3, /device:TPU:1, one launch (start us, length us, event | category | flops | bytes accessed | tf_op | source)
XLA Modules:
  0.0 57.1 jit_solution(14482351896965747703)
XLA Ops:
  1.3 34.8 %shard_map.94 = (f32[2,2,16,16,16]{4,3,2,1,0:T(8,128)}, f32[2,2,32,256]{3,2,1,0:T(8,128)}, f32[2,2,128]{2,1,0:T(2,128)}) custom-call(f32[2,2,16,16,128]{4,3,2,1,0:T(8,128)} %structure_hbm.1, f32[2,2,16,16,16]{4,3,2,1,0:T(8,128)} %medium_hbm.1, s32[1,128]{1,0:T(1,128)} %bitcast.1, s32[1,16]{1,0:T(1,128)} %occupation_hbm.1, f32[1]{0:T(128)S(6)} %copy.10.weight, ...), custom_call_target="tpu_custom_call" | custom-call | tf_op jit(solution)/shard_map/pallas_call | solution.py:675
  36.1 21.0 %shard_map.95 = (f32[2,2,16,16,16]{4,3,2,1,0:T(8,128)}, f32[2,2,32,256]{3,2,1,0:T(8,128)}, f32[2,2,128]{2,1,0:T(2,128)}) custom-call(f32[2,2,16,16,16]{4,3,2,1,0:T(8,128)} %get-tuple-element.6.coarse, f32[2,2,32,256]{3,2,1,0:T(8,128)} %get-tuple-element.7.average, f32[2,2,128]{2,1,0:T(2,128)} %get-tuple-element.8.correction), custom_call_target="tpu_custom_call" | custom-call | tf_op jit(solution)/shard_map/pallas_call | solution.py:703

commit v4 on v3

--- a/solution.py
+++ b/solution.py
@@ -639,13 +639,10 @@
     slot_x.drain(lambda to: block)
 
 
-def output_kernel(coarse, average, correction, coarse_out_ref, average_out, correction_out, sem):
-    pairs = ((coarse, coarse_out_ref), (average, average_out), (correction, correction_out))
-    copies = [pltpu.make_async_copy(a, b, sem.at[at]) for at, (a, b) in enumerate(pairs)]
-    for copy in copies:
-        copy.start()
-    for copy in copies:
-        copy.wait()
+def output_kernel(coarse, average, correction, coarse_to, average_to, correction_to):
+    coarse_to[...] = coarse[...]
+    average_to[...] = average[...]
+    correction_to[...] = correction[...]
 
 
 def shape(*dims):
@@ -703,9 +700,8 @@
     return pl.pallas_call(
         output_kernel,
         out_shape=shapes,
-        in_specs=[any_spec] * 3,
-        out_specs=(any_spec,) * 3,
-        scratch_shapes=[dma((3,))],
+        in_specs=[VMEM_SPEC] * 3,
+        out_specs=(VMEM_SPEC,) * 3,
     )(*results)
 
 

time: 57.2 us -> 38.2 us (0.67)
  Pallas kernels: 55.8 us -> 36.7 us
    pallas_call x1, Pallas kernels: 21 us -> 1.97 us  [per_device(): pl.pallas_call(output_kernel, out_shape=shapes, in_specs=[VMEM_SPEC] * 3,...]
where the time goes in v4:
time: 38.2 us; the launch traced here: 38 us
  Pallas kernels  36.7 us (96%)
  between operations  1.29 us (3%)
    pallas_call x1, Pallas kernels, per_device(): pl.pallas_call(functools.partial(kernel, per_moment, n_ka, n_cfg), out_sh...  34.8 us
    pallas_call x1, Pallas kernels, per_device(): pl.pallas_call(output_kernel, out_shape=shapes, in_specs=[VMEM_SPEC] * 3,...  1.97 us

profile of v4, /device:TPU:1, one launch (start us, length us, event | category | flops | bytes accessed | tf_op | source)
XLA Modules:
  0.0 38.0 jit_solution(12591010169769004914)
XLA Ops:
  1.3 34.8 %shard_map.94 = (f32[2,2,16,16,16]{4,3,2,1,0:T(8,128)}, f32[2,2,32,256]{3,2,1,0:T(8,128)}, f32[2,2,128]{2,1,0:T(2,128)}) custom-call(f32[2,2,16,16,128]{4,3,2,1,0:T(8,128)} %structure_hbm.1, f32[2,2,16,16,16]{4,3,2,1,0:T(8,128)} %medium_hbm.1, s32[1,128]{1,0:T(1,128)} %bitcast.1, s32[1,16]{1,0:T(1,128)} %occupation_hbm.1, f32[1]{0:T(128)S(6)} %copy.10.weight, ...), custom_call_target="tpu_custom_call" | custom-call | tf_op jit(solution)/shard_map/pallas_call | solution.py:672
  36.1 2.0 %shard_map.95 = (f32[2,2,16,16,16]{4,3,2,1,0:T(8,128)}, f32[2,2,32,256]{3,2,1,0:T(8,128)}, f32[2,2,128]{2,1,0:T(2,128)}) custom-call(f32[2,2,16,16,16]{4,3,2,1,0:T(8,128)} %get-tuple-element.6.coarse, f32[2,2,32,256]{3,2,1,0:T(8,128)} %get-tuple-element.7.average, f32[2,2,128]{2,1,0:T(2,128)} %get-tuple-element.8.correction), custom_call_target="tpu_custom_call" | custom-call | tf_op jit(solution)/shard_map/pallas_call | solution.py:700

commit v5 on v4

--- a/solution.py
+++ b/solution.py
@@ -111,21 +111,28 @@
     return block_diag(panel[0], tab), block_diag(panel[1], tab)
 
 
+HELD_ROWS = 8
+
+
 def kpoint_mul(store, left, right):
-    def body(a, carry):
-        re = jnp.zeros((CHANS, LANES), F32)
-        im = jnp.zeros((CHANS, LANES), F32)
+    def body(step, carry):
+        start = step * HELD_ROWS
+        zero = jnp.zeros((CHANS, LANES), F32)
+        p, q, t = [zero] * HELD_ROWS, [zero] * HELD_ROWS, [zero] * HELD_ROWS
         for b in range(CHANS):
-            lr = left[0, a, pl.ds(b, 1), :]
-            li = left[1, a, pl.ds(b, 1), :]
-            rr = right[0, b]
-            ri = right[1, b]
-            re = re + (lr * rr - li * ri)
-            im = im + (lr * ri + li * rr)
-        store(a, re, im)
+            rr, ri = right[0, b], right[1, b]
+            less, more = ri - rr, rr + ri
+            for j in range(HELD_ROWS):
+                lr = left[0, start + j, pl.ds(b, 1), :]
+                li = left[1, start + j, pl.ds(b, 1), :]
+                p[j] = p[j] + (lr + li) * rr
+                q[j] = q[j] + lr * less
+                t[j] = t[j] + li * more
+        for j in range(HELD_ROWS):
+            store(start + j, p[j] - t[j], p[j] + q[j])
         return carry
 
-    lax.fori_loop(0, CHANS, body, 0)
+    lax.fori_loop(0, CHANS // HELD_ROWS, body, 0)
 
 
 def spread_medium(medium, kmap, spread):
@@ -151,25 +158,24 @@
     kpoint_mul(put_h, g, f)
 
 
-def kpoint_sums(inner, kmap, write_tile):
-    rows, lanes = iota((WIDE, LANES), 0), kmap[...]
-    onehot = jnp.transpose(((rows >> 4) == lanes).astype(F32)).astype(BF16)
-    onehot = jnp.concatenate([onehot, onehot], axis=0)
-    row_block = iota((WIDE, WIDE), 0) >> 4
-    col_in = iota((WIDE, WIDE), 1) & 15
-    keep = row_block == col_in
-    for e in range(ENERGIES):
-        for c in range(2):
-            flat = inner[e, c].reshape(WIDE, LANES)
-            parts = jnp.concatenate(split(flat), axis=1)
-            by_mom = jnp.where(keep, dot(parts, onehot), 0.0)
-            panel = jnp.sum(by_mom.reshape(CHANS, CHANS, WIDE), axis=0)
-            for half in range(2):
-                for side in range(2):
-                    write_tile(
-                        ((e * 2 + c) * 2 + half) * 2 + side,
-                        panel[half * 8 : half * 8 + 8, side * LANES : side * LANES + LANES],
-                    )
+def momentum_matrix(kmap):
+    onehot = jnp.transpose(((iota((WIDE, LANES), 0) >> 4) == kmap[...]).astype(F32)).astype(BF16)
+    return jnp.concatenate([onehot, onehot], axis=0)
+
+
+def kpoint_sums(inner, onehot, e, write_tile):
+    keep = (iota((WIDE, WIDE), 0) >> 4) == (iota((WIDE, WIDE), 1) & 15)
+    for c in range(2):
+        flat = inner[e, c].reshape(WIDE, LANES)
+        parts = jnp.concatenate(split(flat), axis=1)
+        by_mom = jnp.where(keep, dot(parts, onehot), 0.0)
+        panel = jnp.sum(by_mom.reshape(CHANS, CHANS, WIDE), axis=0)
+        for half in range(2):
+            for side in range(2):
+                write_tile(
+                    c * 4 + half * 2 + side,
+                    panel[half * 8 : half * 8 + 8, side * LANES : side * LANES + LANES],
+                )
 
 
 def kpoint_squares(spread, factor, tau, square, e):
@@ -458,8 +464,8 @@
 
 
 def gathered_panel(tiles, at):
-    top = jnp.concatenate([tiles[at // 2, 0], tiles[at // 2, 1]], axis=1)
-    low = jnp.concatenate([tiles[at // 2 + 1, 0], tiles[at // 2 + 1, 1]], axis=1)
+    top = jnp.concatenate([tiles[at], tiles[at + 1]], axis=1)
+    low = jnp.concatenate([tiles[at + 2], tiles[at + 3]], axis=1)
     return jnp.concatenate([top, low], axis=0)
 
 
@@ -508,12 +514,12 @@
     coarse, average, correction,
     structure, medium, kmap, occupation, shift_a, shift_b,
     spread, factor, inner, square, panels, rows_tab, shift_tab,
-    row, own_rows, outgoing, first, part, total, block, slots,
+    row, own_rows, outgoing, first, part_a, part_b, total, block, slots,
     load_sem, row_send, row_recv, first_send, first_recv, part_send, part_recv,
     total_send, total_recv, slot_send, slot_recv,
 ):
     pairs = (
-        (medium_hbm, medium), (kmap_hbm, kmap), (structure_hbm, structure),
+        (kmap_hbm, kmap), (medium_hbm, medium), (structure_hbm, structure),
         (occupation_hbm, occupation), (shift_a_hbm, shift_a), (shift_b_hbm, shift_b),
     )
     loads = [
@@ -522,13 +528,60 @@
     for load in loads:
         load.start()
     barrier = greet(n_ka, n_cfg)
+    energies = range(ENERGIES)
+    parts = (part_a, part_b)
     rows_x = Exchange("cfg", n_cfg, own_rows, row_send, row_recv)
-    first_x = Exchange("cfg", n_cfg, first, first_send, first_recv)
-    part_x = Exchange("ka", n_ka, part, part_send, part_recv)
-    total_x = Exchange("cfg", n_cfg, total, total_send, total_recv)
-    slot_x = Exchange("ka", n_ka, slots, slot_send, slot_recv)
-    ka, cfg = part_x.me, rows_x.me
+    first_x = [
+        Exchange("cfg", n_cfg, first.at[e], first_send.at[e], first_recv.at[e]) for e in energies
+    ]
+    part_x = [Exchange("ka", n_ka, parts[e], part_send.at[e], part_recv.at[e]) for e in energies]
+    total_x = [
+        Exchange("cfg", n_cfg, total.at[e], total_send.at[e], total_recv.at[e]) for e in energies
+    ]
+    slot_x = [Exchange("ka", n_ka, slots.at[e], slot_send.at[e], slot_recv.at[e]) for e in energies]
+    ka, cfg = lax.axis_index("ka"), lax.axis_index("cfg")
+
+    def own_row(to):
+        return row
+
+    def own_sums(e):
+        return lambda to: outgoing.at[e, to]
+
+    def own_part(e):
+        return lambda to: parts[e].at[ka]
+
+    def own_total(e):
+        return lambda to: total.at[e, cfg]
+
+    def own_block(e):
+        return lambda to: block.at[e]
+
+    def send_sums(e):
+        def write(at, value):
+            outgoing[e, at] = value
+
+        kpoint_sums(inner, onehot, e, write)
+        first_x[e].start(own_sums(e))
+        first[e, cfg] = outgoing[e, cfg]
+
+    def send_part(e):
+        first_x[e].wait(own_sums(e))
+        value = first[e, 0]
+        for at in range(1, n_cfg):
+            value = value + first[e, at]
+        parts[e][ka, 0] = value
+        part_x[e].start(own_part(e))
+
+    def send_total(e):
+        part_x[e].wait(own_part(e))
+        value = parts[e][0, 0]
+        for at in range(1, n_ka):
+            value = value + parts[e][at, 0]
+        total[e, cfg] = value
+        total_x[e].start(own_total(e))
+
     loads[0].wait()
+    onehot = momentum_matrix(kmap)
     loads[1].wait()
     spread_medium(medium, kmap, spread)
     loads[2].wait()
@@ -537,33 +590,20 @@
         load.wait()
     config_row(occupation, weight, row)
     pl.semaphore_wait(barrier, n_ka + n_cfg - 2)
-    rows_x.start(lambda to: row)
+    rows_x.start(own_row)
     own_rows[cfg] = row[...]
+    send_sums(0)
     kpoint_inner(structure, spread, factor, inner, 1)
-
-    def write(at, value):
-        outgoing[at // 2, at % 2] = value
-
-    kpoint_sums(inner, kmap, write)
-    first_x.start(lambda to: outgoing.at[to])
-    first[cfg] = outgoing[cfg]
+    send_sums(1)
     kpoint_squares(spread, factor, inner, square, 0)
-    rows_x.wait(lambda to: row)
+    rows_x.wait(own_row)
     line = iota((8, LANES), 0)
     group = jnp.zeros((8, LANES), F32)
     for at in range(n_cfg):
         group = group + jnp.where(line == at, own_rows[at], 0.0)
-    first_x.wait(lambda to: outgoing.at[to])
-    value = [first[0, 0], first[0, 1]]
-    for at in range(1, n_cfg):
-        value = [value[0] + first[at, 0], value[1] + first[at, 1]]
-    part[ka, 0] = value[0]
-    part[ka, 1] = value[1]
-    part[ka, 2] = group
-    part_x.start(lambda to: part.at[ka])
-    kpoint_squares(spread, factor, inner, square, 1)
+    part_a[ka, 1] = group
+    send_part(0)
     tab = Tables()
-    energies = range(ENERGIES)
     y = [medium_panels(medium, tab, e) for e in energies]
     wide = [shift_panels(shift_a, shift_b, tab, e) for e in energies]
     y_b = [cdot(y[e], block_diag_c(wide[e][0], tab)) for e in energies]
@@ -572,21 +612,16 @@
         (block_diag_c(y[e], tab), block_diag_c(y_b[e], tab), block_diag_c(y_c[e], tab))
         for e in energies
     ]
-    part_x.wait(lambda to: part.at[ka])
-    value = [part[0, 0], part[0, 1]]
-    for at in range(1, n_ka):
-        value = [value[0] + part[at, 0], value[1] + part[at, 1]]
-    total[cfg, 0] = value[0]
-    total[cfg, 1] = value[1]
-    total_x.start(lambda to: total.at[cfg])
-    configs = jnp.concatenate([part[at, 2] for at in range(n_ka)], axis=0)
+    send_part(1)
+    kpoint_squares(spread, factor, inner, square, 1)
+    send_total(0)
+    configs = jnp.concatenate([part_a[at, 1] for at in range(n_ka)], axis=0)
     moment_tables(configs, tab, rows_tab, shift_tab)
-    total_x.wait(lambda to: total.at[cfg])
-    which = iota((8, WIDE), 0)
-    out = jnp.zeros((8, WIDE), F32)
+    send_total(1)
     kept = []
     for e in energies:
-        sum_t = (gathered_panel(total, e * 8), gathered_panel(total, e * 8 + 4))
+        total_x[e].wait(own_total(e))
+        sum_t = (gathered_panel(total.at[e], 0), gathered_panel(total.at[e], 4))
         x, x_b, x_c = coarse_panels(y[e], y_b[e], y_c[e], y_all[e], sum_t, tab, per_moment)
         lines = []
         for at, panel in enumerate((x, x_b, x_c)):
@@ -602,14 +637,17 @@
         tb_parts = translated_c(top_b)[1]
         tc_full, tc_parts = translated_c(top_c)
         avg = rows_stage(start, with_b, with_c, t_parts, tb_parts, tc_parts, rows_tab)
+        out = jnp.zeros((8, LANES), F32)
         for c in range(2):
             for site in range(2):
-                at = e * 4 + c * 2 + site
-                out = jnp.where(which == at, avg[c][site * 8 : site * 8 + 8], out)
+                for side in range(2):
+                    at = c * 4 + site * 2 + side
+                    lanes = avg[c][site * 8 : site * 8 + 8, side * LANES : side * LANES + LANES]
+                    out = jnp.where(line == at, lanes, out)
+        block[e] = out
+        slot_x[e].start(own_block(e))
+        slots[e, ka] = out
         kept.append((top_b, top_c, tc_full, tb_parts, tc_parts, x))
-    block[...] = out
-    slot_x.start(lambda to: block)
-    slots[ka] = out
     for e in energies:
         x = kept[e][5]
         d = moment_stage(
@@ -624,19 +662,23 @@
                 coarse[e, c] = value
 
             coarse_out(x[c], tab, store)
-    slot_x.wait(lambda to: block)
-    for at in range(n_ka):
-        for e in energies:
+    for e in energies:
+        slot_x[e].wait(own_block(e))
+        for at in range(n_ka):
             for c in range(2):
                 for site in range(2):
-                    line = e * 4 + c * 2 + site
-                    to = site * CHANS + at
-                    average[e, c, to : to + 1, :] = slots[at, line : line + 1, :]
-    rows_x.drain(lambda to: row)
-    first_x.drain(lambda to: outgoing.at[to])
-    part_x.drain(lambda to: part.at[ka])
-    total_x.drain(lambda to: total.at[cfg])
-    slot_x.drain(lambda to: block)
+                    for side in range(2):
+                        of = c * 4 + site * 2 + side
+                        to = site * CHANS + at
+                        average[e, c, to : to + 1, side * LANES : side * LANES + LANES] = slots[
+                            e, at, of : of + 1, :
+                        ]
+    rows_x.drain(own_row)
+    for e in energies:
+        first_x[e].drain(own_sums(e))
+        part_x[e].drain(own_part(e))
+        total_x[e].drain(own_total(e))
+        slot_x[e].drain(own_block(e))
 
 
 def output_kernel(coarse, average, correction, coarse_to, average_to, correction_to):
@@ -683,15 +725,16 @@
             vmem(SITES + 1, ALPHA, WIDE + LANES),
             vmem(2, WIDE, WIDE),
             vmem(8, LANES), vmem(n_cfg, 8, LANES),
-            vmem(n_cfg, 2, 8, LANES), vmem(n_cfg, 2, 8, LANES),
-            vmem(n_ka, 3, 8, LANES), vmem(n_cfg, 2, 8, LANES),
-            vmem(8, WIDE), vmem(n_ka, 8, WIDE),
+            vmem(ENERGIES, n_cfg, 8, LANES), vmem(ENERGIES, n_cfg, 8, LANES),
+            vmem(n_ka, 2, 8, LANES), vmem(n_ka, 1, 8, LANES),
+            vmem(ENERGIES, n_cfg, 8, LANES),
+            vmem(ENERGIES, 8, LANES), vmem(ENERGIES, n_ka, 8, LANES),
             dma((6,)),
             dma((n_cfg,)), dma((n_cfg,)),
-            dma((n_cfg,)), dma((n_cfg,)),
-            dma((n_ka,)), dma((n_ka,)),
-            dma((n_cfg,)), dma((n_cfg,)),
-            dma((n_ka,)), dma((n_ka,)),
+            dma((ENERGIES, n_cfg)), dma((ENERGIES, n_cfg)),
+            dma((ENERGIES, n_ka)), dma((ENERGIES, n_ka)),
+            dma((ENERGIES, n_cfg)), dma((ENERGIES, n_cfg)),
+            dma((ENERGIES, n_ka)), dma((ENERGIES, n_ka)),
         ],
         compiler_params=pltpu.CompilerParams(
             collective_id=0, has_side_effects=True, vmem_limit_bytes=56 * 1024 * 1024

time: 38.2 us -> 37.5 us (0.982)
  Pallas kernels: 36.7 us -> 36.1 us
    pallas_call x1, Pallas kernels: 34.8 us -> 34.1 us  [per_device(): pl.pallas_call(functools.partial(kernel, per_moment, n_ka, n_cfg), out_sh...]
where the time goes in v5:
time: 37.5 us; the launch traced here: 37.4 us
  Pallas kernels  36.1 us (96%)
  between operations  1.29 us (3%)
    pallas_call x1, Pallas kernels, per_device(): pl.pallas_call(functools.partial(kernel, per_moment, n_ka, n_cfg), out_sh...  34.1 us
    pallas_call x1, Pallas kernels, per_device(): pl.pallas_call(output_kernel, out_shape=shapes, in_specs=[VMEM_SPEC] * 3,...  1.97 us

profile of v5, /device:TPU:1, one launch (start us, length us, event | category | flops | bytes accessed | tf_op | source)
XLA Modules:
  0.0 37.4 jit_solution(2927132852156148519)
XLA Ops:
  1.3 34.1 %shard_map.94 = (f32[2,2,16,16,16]{4,3,2,1,0:T(8,128)}, f32[2,2,32,256]{3,2,1,0:T(8,128)}, f32[2,2,128]{2,1,0:T(2,128)}) custom-call(f32[2,2,16,16,128]{4,3,2,1,0:T(8,128)} %structure_hbm.1, f32[2,2,16,16,16]{4,3,2,1,0:T(8,128)} %medium_hbm.1, s32[1,128]{1,0:T(1,128)} %bitcast.1, s32[1,16]{1,0:T(1,128)} %occupation_hbm.1, f32[1]{0:T(128)S(6)} %copy.10.weight, ...), custom_call_target="tpu_custom_call" | custom-call | tf_op jit(solution)/shard_map/pallas_call | solution.py:714
  35.4 2.0 %shard_map.95 = (f32[2,2,16,16,16]{4,3,2,1,0:T(8,128)}, f32[2,2,32,256]{3,2,1,0:T(8,128)}, f32[2,2,128]{2,1,0:T(2,128)}) custom-call(f32[2,2,16,16,16]{4,3,2,1,0:T(8,128)} %get-tuple-element.6.coarse, f32[2,2,32,256]{3,2,1,0:T(8,128)} %get-tuple-element.7.average, f32[2,2,128]{2,1,0:T(2,128)} %get-tuple-element.8.correction), custom_call_target="tpu_custom_call" | custom-call | tf_op jit(solution)/shard_map/pallas_call | solution.py:743

commit v6 on v5

--- a/solution.py
+++ b/solution.py
@@ -143,19 +143,24 @@
             spread[e, c] = dot_exact(flat, onehot).reshape(CHANS, CHANS, LANES)
 
 
-def kpoint_inner(structure, spread, factor, inner, e):
-    y, g, f, h = spread.at[e], structure.at[e], factor.at[e], inner.at[e]
-
-    def put_f(a, re, im):
+def kpoint_factor(structure, spread, factor, e):
+    f = factor.at[e]
+
+    def put(a, re, im):
         f[0, a] = re
         f[1, a] = im
 
-    def put_h(a, re, im):
+    kpoint_mul(put, spread.at[e], structure.at[e])
+
+
+def kpoint_inner(structure, factor, inner, e):
+    g, h = structure.at[e], inner.at[e]
+
+    def put(a, re, im):
         h[0, a] = g[0, a] + re
         h[1, a] = g[1, a] + im
 
-    kpoint_mul(put_f, y, g)
-    kpoint_mul(put_h, g, f)
+    kpoint_mul(put, g, factor.at[e])
 
 
 def momentum_matrix(kmap):
@@ -469,43 +474,58 @@
     return jnp.concatenate([top, low], axis=0)
 
 
+def offsets(outer, inner, torus):
+    def hops(step):
+        first = min(step[0], outer - step[0])
+        return first + (min(step[1], inner - step[1]) if torus else 0.5 * (step[1] > 0))
+
+    steps = [(a, b) for a in range(outer) for b in range(inner) if a or b]
+    return sorted(steps, key=lambda step: (-hops(step), step))
+
+
+class Group:
+    def __init__(self, axis, inner, torus):
+        self.axis, self.inner = axis, inner
+        self.count = lax.axis_size(axis)
+        self.outer = self.count // inner
+        self.steps = offsets(self.outer, inner, torus)
+        self.me = lax.axis_index(axis)
+
+    def peer(self, step):
+        first = lax.rem(self.me // self.inner + step[0], self.outer)
+        return first * self.inner + lax.rem(lax.rem(self.me, self.inner) + step[1], self.inner)
+
+    def greet(self, barrier):
+        for step in self.steps:
+            pl.semaphore_signal(
+                barrier, inc=1, device_id={self.axis: self.peer(step)}, device_id_type=MESH
+            )
+
+
 class Exchange:
-    def __init__(self, axis, count, slots, send, recv):
-        self.axis, self.count = axis, count
-        self.slots, self.send, self.recv = slots, send, recv
-        self.me = lax.axis_index(axis)
-
-    def peer(self, d):
-        return lax.rem(self.me + d, self.count)
-
-    def copy(self, src, at, d):
+    def __init__(self, group, slots, send, recv):
+        self.group, self.slots, self.send, self.recv = group, slots, send, recv
+
+    def copy(self, src, at, number, peer):
         return pltpu.make_async_remote_copy(
-            src_ref=src, dst_ref=self.slots.at[at], send_sem=self.send.at[d],
-            recv_sem=self.recv.at[at], device_id={self.axis: self.peer(d)}, device_id_type=MESH,
+            src_ref=src, dst_ref=self.slots.at[at], send_sem=self.send.at[number],
+            recv_sem=self.recv.at[at], device_id={self.group.axis: peer}, device_id_type=MESH,
         )
 
     def start(self, source):
-        for d in range(1, self.count):
-            self.copy(source(self.peer(d)), self.me, d).start()
+        for number, step in enumerate(self.group.steps):
+            peer = self.group.peer(step)
+            self.copy(source(peer), self.group.me, number, peer).start()
 
     def wait(self, source):
-        for d in range(1, self.count):
-            self.copy(source(self.me), self.peer(d), d).wait_recv()
+        for number, step in enumerate(self.group.steps[::-1]):
+            peer = self.group.peer(step)
+            self.copy(source(self.group.me), peer, number, peer).wait_recv()
 
     def drain(self, source):
-        for d in range(1, self.count):
-            self.copy(source(self.me), self.me, d).wait_send()
-
-
-def greet(n_ka, n_cfg):
-    barrier = pltpu.get_barrier_semaphore()
-    for axis, count in (("ka", n_ka), ("cfg", n_cfg)):
-        me = lax.axis_index(axis)
-        for d in range(1, count):
-            pl.semaphore_signal(
-                barrier, inc=1, device_id={axis: lax.rem(me + d, count)}, device_id_type=MESH
-            )
-    return barrier
+        for number, step in enumerate(self.group.steps):
+            peer = self.group.peer(step)
+            self.copy(source(self.group.me), self.group.me, number, peer).wait_send()
 
 
 def kernel(
@@ -525,20 +545,21 @@
     loads = [
         pltpu.make_async_copy(source, to, load_sem.at[at]) for at, (source, to) in enumerate(pairs)
     ]
-    for load in loads:
+    for load in loads[:3]:
         load.start()
-    barrier = greet(n_ka, n_cfg)
+    barrier = pltpu.get_barrier_semaphore()
+    by_ka, by_cfg = Group("ka", 4, True), Group("cfg", 2, False)
+    by_ka.greet(barrier)
+    by_cfg.greet(barrier)
+    for load in loads[3:]:
+        load.start()
     energies = range(ENERGIES)
     parts = (part_a, part_b)
-    rows_x = Exchange("cfg", n_cfg, own_rows, row_send, row_recv)
-    first_x = [
-        Exchange("cfg", n_cfg, first.at[e], first_send.at[e], first_recv.at[e]) for e in energies
-    ]
-    part_x = [Exchange("ka", n_ka, parts[e], part_send.at[e], part_recv.at[e]) for e in energies]
-    total_x = [
-        Exchange("cfg", n_cfg, total.at[e], total_send.at[e], total_recv.at[e]) for e in energies
-    ]
-    slot_x = [Exchange("ka", n_ka, slots.at[e], slot_send.at[e], slot_recv.at[e]) for e in energies]
+    rows_x = Exchange(by_cfg, own_rows, row_send, row_recv)
+    first_x = [Exchange(by_cfg, first.at[e], first_send.at[e], first_recv.at[e]) for e in energies]
+    part_x = [Exchange(by_ka, parts[e], part_send.at[e], part_recv.at[e]) for e in energies]
+    total_x = [Exchange(by_cfg, total.at[e], total_send.at[e], total_recv.at[e]) for e in energies]
+    slot_x = [Exchange(by_ka, slots.at[e], slot_send.at[e], slot_recv.at[e]) for e in energies]
     ka, cfg = lax.axis_index("ka"), lax.axis_index("cfg")
 
     def own_row(to):
@@ -556,11 +577,13 @@
     def own_block(e):
         return lambda to: block.at[e]
 
-    def send_sums(e):
+    def make_sums(e):
         def write(at, value):
             outgoing[e, at] = value
 
         kpoint_sums(inner, onehot, e, write)
+
+    def send_sums(e):
         first_x[e].start(own_sums(e))
         first[e, cfg] = outgoing[e, cfg]
 
@@ -585,16 +608,20 @@
     loads[1].wait()
     spread_medium(medium, kmap, spread)
     loads[2].wait()
-    kpoint_inner(structure, spread, factor, inner, 0)
+    kpoint_factor(structure, spread, factor, 0)
+    kpoint_inner(structure, factor, inner, 0)
+    make_sums(0)
+    kpoint_factor(structure, spread, factor, 1)
     for load in loads[3:]:
         load.wait()
     config_row(occupation, weight, row)
     pl.semaphore_wait(barrier, n_ka + n_cfg - 2)
+    send_sums(0)
+    kpoint_inner(structure, factor, inner, 1)
+    make_sums(1)
+    send_sums(1)
     rows_x.start(own_row)
     own_rows[cfg] = row[...]
-    send_sums(0)
-    kpoint_inner(structure, spread, factor, inner, 1)
-    send_sums(1)
     kpoint_squares(spread, factor, inner, square, 0)
     rows_x.wait(own_row)
     line = iota((8, LANES), 0)

time: 37.5 us -> 37 us (0.987)
  Pallas kernels: 36.1 us -> 35.6 us
    pallas_call x1, Pallas kernels: 34.1 us -> 33.6 us  [per_device(): pl.pallas_call(functools.partial(kernel, per_moment, n_ka, n_cfg), out_sh...]
where the time goes in v6:
time: 37 us; the launch traced here: 36.9 us
  Pallas kernels  35.6 us (96%)
  between operations  1.29 us (3%)
    pallas_call x1, Pallas kernels, per_device(): pl.pallas_call(functools.partial(kernel, per_moment, n_ka, n_cfg), out_sh...  33.6 us
    pallas_call x1, Pallas kernels, per_device(): pl.pallas_call(output_kernel, out_shape=shapes, in_specs=[VMEM_SPEC] * 3,...  1.97 us

profile of v6, /device:TPU:1, one launch (start us, length us, event | category | flops | bytes accessed | tf_op | source)
XLA Modules:
  0.0 36.9 jit_solution(15209032455880839690)
XLA Ops:
  1.3 33.6 %shard_map.94 = (f32[2,2,16,16,16]{4,3,2,1,0:T(8,128)}, f32[2,2,32,256]{3,2,1,0:T(8,128)}, f32[2,2,128]{2,1,0:T(2,128)}) custom-call(f32[2,2,16,16,128]{4,3,2,1,0:T(8,128)} %structure_hbm.1, f32[2,2,16,16,16]{4,3,2,1,0:T(8,128)} %medium_hbm.1, s32[1,128]{1,0:T(1,128)} %bitcast.1, s32[1,16]{1,0:T(1,128)} %occupation_hbm.1, f32[1]{0:T(128)S(6)} %copy.10.weight, ...), custom_call_target="tpu_custom_call" | custom-call | tf_op jit(solution)/shard_map/pallas_call | solution.py:741
  34.9 2.0 %shard_map.95 = (f32[2,2,16,16,16]{4,3,2,1,0:T(8,128)}, f32[2,2,32,256]{3,2,1,0:T(8,128)}, f32[2,2,128]{2,1,0:T(2,128)}) custom-call(f32[2,2,16,16,16]{4,3,2,1,0:T(8,128)} %get-tuple-element.6.coarse, f32[2,2,32,256]{3,2,1,0:T(8,128)} %get-tuple-element.7.average, f32[2,2,128]{2,1,0:T(2,128)} %get-tuple-element.8.correction), custom_call_target="tpu_custom_call" | custom-call | tf_op jit(solution)/shard_map/pallas_call | solution.py:770

commit v7 on v6

--- a/solution.py
+++ b/solution.py
@@ -534,7 +534,7 @@
     coarse, average, correction,
     structure, medium, kmap, occupation, shift_a, shift_b,
     spread, factor, inner, square, panels, rows_tab, shift_tab,
-    row, own_rows, outgoing, first, part_a, part_b, total, block, slots,
+    row, own_rows, outgoing, first, part, total, block, slots,
     load_sem, row_send, row_recv, first_send, first_recv, part_send, part_recv,
     total_send, total_recv, slot_send, slot_recv,
 ):
@@ -554,72 +554,47 @@
     for load in loads[3:]:
         load.start()
     energies = range(ENERGIES)
-    parts = (part_a, part_b)
     rows_x = Exchange(by_cfg, own_rows, row_send, row_recv)
-    first_x = [Exchange(by_cfg, first.at[e], first_send.at[e], first_recv.at[e]) for e in energies]
-    part_x = [Exchange(by_ka, parts[e], part_send.at[e], part_recv.at[e]) for e in energies]
-    total_x = [Exchange(by_cfg, total.at[e], total_send.at[e], total_recv.at[e]) for e in energies]
-    slot_x = [Exchange(by_ka, slots.at[e], slot_send.at[e], slot_recv.at[e]) for e in energies]
+    first_x = Exchange(by_cfg, first, first_send, first_recv)
+    part_x = Exchange(by_ka, part, part_send, part_recv)
+    total_x = Exchange(by_cfg, total, total_send, total_recv)
+    slot_x = Exchange(by_ka, slots, slot_send, slot_recv)
     ka, cfg = lax.axis_index("ka"), lax.axis_index("cfg")
 
     def own_row(to):
         return row
 
-    def own_sums(e):
-        return lambda to: outgoing.at[e, to]
-
-    def own_part(e):
-        return lambda to: parts[e].at[ka]
-
-    def own_total(e):
-        return lambda to: total.at[e, cfg]
-
-    def own_block(e):
-        return lambda to: block.at[e]
-
-    def make_sums(e):
-        def write(at, value):
-            outgoing[e, at] = value
-
-        kpoint_sums(inner, onehot, e, write)
-
-    def send_sums(e):
-        first_x[e].start(own_sums(e))
-        first[e, cfg] = outgoing[e, cfg]
-
-    def send_part(e):
-        first_x[e].wait(own_sums(e))
-        value = first[e, 0]
-        for at in range(1, n_cfg):
-            value = value + first[e, at]
-        parts[e][ka, 0] = value
-        part_x[e].start(own_part(e))
-
-    def send_total(e):
-        part_x[e].wait(own_part(e))
-        value = parts[e][0, 0]
-        for at in range(1, n_ka):
-            value = value + parts[e][at, 0]
-        total[e, cfg] = value
-        total_x[e].start(own_total(e))
+    def own_sums(to):
+        return outgoing.at[to]
+
+    def own_part(to):
+        return part.at[ka]
+
+    def own_total(to):
+        return total.at[cfg]
+
+    def own_block(to):
+        return block
 
     loads[0].wait()
     onehot = momentum_matrix(kmap)
     loads[1].wait()
     spread_medium(medium, kmap, spread)
     loads[2].wait()
-    kpoint_factor(structure, spread, factor, 0)
-    kpoint_inner(structure, factor, inner, 0)
-    make_sums(0)
-    kpoint_factor(structure, spread, factor, 1)
+    for e in energies:
+        kpoint_factor(structure, spread, factor, e)
+        kpoint_inner(structure, factor, inner, e)
+
+        def write(at, value, e=e):
+            outgoing[at, e] = value
+
+        kpoint_sums(inner, onehot, e, write)
     for load in loads[3:]:
         load.wait()
     config_row(occupation, weight, row)
     pl.semaphore_wait(barrier, n_ka + n_cfg - 2)
-    send_sums(0)
-    kpoint_inner(structure, factor, inner, 1)
-    make_sums(1)
-    send_sums(1)
+    first_x.start(own_sums)
+    first[cfg] = outgoing[cfg]
     rows_x.start(own_row)
     own_rows[cfg] = row[...]
     kpoint_squares(spread, factor, inner, square, 0)
@@ -628,8 +603,14 @@
     group = jnp.zeros((8, LANES), F32)
     for at in range(n_cfg):
         group = group + jnp.where(line == at, own_rows[at], 0.0)
-    part_a[ka, 1] = group
-    send_part(0)
+    first_x.wait(own_sums)
+    for e in energies:
+        value = first[0, e]
+        for at in range(1, n_cfg):
+            value = value + first[at, e]
+        part[ka, e] = value
+    part[ka, ENERGIES] = group
+    part_x.start(own_part)
     tab = Tables()
     y = [medium_panels(medium, tab, e) for e in energies]
     wide = [shift_panels(shift_a, shift_b, tab, e) for e in energies]
@@ -639,48 +620,63 @@
         (block_diag_c(y[e], tab), block_diag_c(y_b[e], tab), block_diag_c(y_c[e], tab))
         for e in energies
     ]
-    send_part(1)
     kpoint_squares(spread, factor, inner, square, 1)
-    send_total(0)
-    configs = jnp.concatenate([part_a[at, 1] for at in range(n_ka)], axis=0)
+    part_x.wait(own_part)
+    for e in energies:
+        value = part[0, e]
+        for at in range(1, n_ka):
+            value = value + part[at, e]
+        total[cfg, e] = value
+    total_x.start(own_total)
+    configs = jnp.concatenate([part[at, ENERGIES] for at in range(n_ka)], axis=0)
     moment_tables(configs, tab, rows_tab, shift_tab)
-    send_total(1)
-    kept = []
+    total_x.wait(own_total)
+    found = []
     for e in energies:
-        total_x[e].wait(own_total(e))
-        sum_t = (gathered_panel(total.at[e], 0), gathered_panel(total.at[e], 4))
-        x, x_b, x_c = coarse_panels(y[e], y_b[e], y_c[e], y_all[e], sum_t, tab, per_moment)
+        tiles = [total[at, e] for at in range(n_cfg)]
+        sum_t = (gathered_panel(tiles, 0), gathered_panel(tiles, 4))
+        found.append(coarse_panels(y[e], y_b[e], y_c[e], y_all[e], sum_t, tab, per_moment))
+    rows = []
+    for e in energies:
         lines = []
-        for at, panel in enumerate((x, x_b, x_c)):
+        for at, panel in enumerate(found[e]):
             panels[e, at, 0] = panel[0]
             panels[e, at, 1] = panel[1]
             lines.append(
                 (panels[e, at, 0, pl.ds(ka, 1), :], panels[e, at, 1, pl.ds(ka, 1), :])
             )
-        (top, start), (top_b, with_b), (top_c, with_c) = first_rows(
-            (x, x_b, x_c), lines, tab, cfg * 2
+        rows.append(first_rows(found[e], lines, tab, cfg * 2))
+    t_all = [translated_c(rows[e][0][0])[1] for e in energies]
+    tb_all = [translated_c(rows[e][1][0])[1] for e in energies]
+    tc_all = [translated_c(rows[e][2][0]) for e in energies]
+    averages = [
+        rows_stage(
+            rows[e][0][1], rows[e][1][1], rows[e][2][1], t_all[e], tb_all[e], tc_all[e][1], rows_tab
         )
-        t_parts = translated_c(top)[1]
-        tb_parts = translated_c(top_b)[1]
-        tc_full, tc_parts = translated_c(top_c)
-        avg = rows_stage(start, with_b, with_c, t_parts, tb_parts, tc_parts, rows_tab)
+        for e in energies
+    ]
+    for e in energies:
         out = jnp.zeros((8, LANES), F32)
         for c in range(2):
             for site in range(2):
                 for side in range(2):
                     at = c * 4 + site * 2 + side
-                    lanes = avg[c][site * 8 : site * 8 + 8, side * LANES : side * LANES + LANES]
+                    lanes = averages[e][c][
+                        site * 8 : site * 8 + 8, side * LANES : side * LANES + LANES
+                    ]
                     out = jnp.where(line == at, lanes, out)
         block[e] = out
-        slot_x[e].start(own_block(e))
-        slots[e, ka] = out
-        kept.append((top_b, top_c, tc_full, tb_parts, tc_parts, x))
+    slot_x.start(own_block)
+    slots[ka] = block[...]
+    moments = [
+        moment_stage(
+            rows[e][1][0], rows[e][2][0], tc_all[e][0], tb_all[e], tc_all[e][1], found[e][0],
+            block_diag_c(found[e][0], tab), wide[e][0], wide[e][1], shift_tab, tab,
+        )
+        for e in energies
+    ]
     for e in energies:
-        x = kept[e][5]
-        d = moment_stage(
-            *kept[e], block_diag_c(x, tab), wide[e][0], wide[e][1], shift_tab, tab
-        )
-        re, im = correction_stage(d, square, e, kmap, tab)
+        re, im = correction_stage(moments[e], square, e, kmap, tab)
         correction[e, 0:1, :] = re
         correction[e, 1:2, :] = im
         for c in range(2):
@@ -688,9 +684,9 @@
             def store(value, e=e, c=c):
                 coarse[e, c] = value
 
-            coarse_out(x[c], tab, store)
+            coarse_out(found[e][0][c], tab, store)
+    slot_x.wait(own_block)
     for e in energies:
-        slot_x[e].wait(own_block(e))
         for at in range(n_ka):
             for c in range(2):
                 for site in range(2):
@@ -698,14 +694,13 @@
                         of = c * 4 + site * 2 + side
                         to = site * CHANS + at
                         average[e, c, to : to + 1, side * LANES : side * LANES + LANES] = slots[
-                            e, at, of : of + 1, :
+                            at, e, of : of + 1, :
                         ]
     rows_x.drain(own_row)
-    for e in energies:
-        first_x[e].drain(own_sums(e))
-        part_x[e].drain(own_part(e))
-        total_x[e].drain(own_total(e))
-        slot_x[e].drain(own_block(e))
+    first_x.drain(own_sums)
+    part_x.drain(own_part)
+    total_x.drain(own_total)
+    slot_x.drain(own_block)
 
 
 def output_kernel(coarse, average, correction, coarse_to, average_to, correction_to):
@@ -752,16 +747,16 @@
             vmem(SITES + 1, ALPHA, WIDE + LANES),
             vmem(2, WIDE, WIDE),
             vmem(8, LANES), vmem(n_cfg, 8, LANES),
-            vmem(ENERGIES, n_cfg, 8, LANES), vmem(ENERGIES, n_cfg, 8, LANES),
-            vmem(n_ka, 2, 8, LANES), vmem(n_ka, 1, 8, LANES),
-            vmem(ENERGIES, n_cfg, 8, LANES),
-            vmem(ENERGIES, 8, LANES), vmem(ENERGIES, n_ka, 8, LANES),
+            vmem(n_cfg, ENERGIES, 8, LANES), vmem(n_cfg, ENERGIES, 8, LANES),
+            vmem(n_ka, ENERGIES + 1, 8, LANES),
+            vmem(n_cfg, ENERGIES, 8, LANES),
+            vmem(ENERGIES, 8, LANES), vmem(n_ka, ENERGIES, 8, LANES),
             dma((6,)),
             dma((n_cfg,)), dma((n_cfg,)),
-            dma((ENERGIES, n_cfg)), dma((ENERGIES, n_cfg)),
-            dma((ENERGIES, n_ka)), dma((ENERGIES, n_ka)),
-            dma((ENERGIES, n_cfg)), dma((ENERGIES, n_cfg)),
-            dma((ENERGIES, n_ka)), dma((ENERGIES, n_ka)),
+            dma((n_cfg,)), dma((n_cfg,)),
+            dma((n_ka,)), dma((n_ka,)),
+            dma((n_cfg,)), dma((n_cfg,)),
+            dma((n_ka,)), dma((n_ka,)),
         ],
         compiler_params=pltpu.CompilerParams(
             collective_id=0, has_side_effects=True, vmem_limit_bytes=56 * 1024 * 1024

time: 37 us -> 35.3 us (0.954)
  Pallas kernels: 35.6 us -> 33.8 us
    pallas_call x1, Pallas kernels: 33.6 us -> 31.8 us  [per_device(): pl.pallas_call(functools.partial(kernel, per_moment, n_ka, n_cfg), out_sh...]
where the time goes in v7:
time: 35.3 us; the launch traced here: 35.1 us
  Pallas kernels  33.8 us (96%)
  between operations  1.29 us (4%)
    pallas_call x1, Pallas kernels, per_device(): pl.pallas_call(functools.partial(kernel, per_moment, n_ka, n_cfg), out_sh...  31.8 us
    pallas_call x1, Pallas kernels, per_device(): pl.pallas_call(output_kernel, out_shape=shapes, in_specs=[VMEM_SPEC] * 3,...  1.97 us

profile of v7, /device:TPU:1, one launch (start us, length us, event | category | flops | bytes accessed | tf_op | source)
XLA Modules:
  0.0 35.1 jit_solution(4399311740738976778)
XLA Ops:
  1.3 31.8 %shard_map.94 = (f32[2,2,16,16,16]{4,3,2,1,0:T(8,128)}, f32[2,2,32,256]{3,2,1,0:T(8,128)}, f32[2,2,128]{2,1,0:T(2,128)}) custom-call(f32[2,2,16,16,128]{4,3,2,1,0:T(8,128)} %structure_hbm.1, f32[2,2,16,16,16]{4,3,2,1,0:T(8,128)} %medium_hbm.1, s32[1,128]{1,0:T(1,128)} %bitcast.1, s32[1,16]{1,0:T(1,128)} %occupation_hbm.1, f32[1]{0:T(128)S(6)} %copy.10.weight, ...), custom_call_target="tpu_custom_call" | custom-call | tf_op jit(solution)/shard_map/pallas_call | solution.py:736
  33.1 2.0 %shard_map.95 = (f32[2,2,16,16,16]{4,3,2,1,0:T(8,128)}, f32[2,2,32,256]{3,2,1,0:T(8,128)}, f32[2,2,128]{2,1,0:T(2,128)}) custom-call(f32[2,2,16,16,16]{4,3,2,1,0:T(8,128)} %get-tuple-element.6.coarse, f32[2,2,32,256]{3,2,1,0:T(8,128)} %get-tuple-element.7.average, f32[2,2,128]{2,1,0:T(2,128)} %get-tuple-element.8.correction), custom_call_target="tpu_custom_call" | custom-call | tf_op jit(solution)/shard_map/pallas_call | solution.py:765

commit v8 on v7

--- a/solution.py
+++ b/solution.py
@@ -531,11 +531,11 @@
 def kernel(
     per_moment, n_ka, n_cfg,
     structure_hbm, medium_hbm, kmap_hbm, occupation_hbm, weight, shift_a_hbm, shift_b_hbm,
-    coarse, average, correction,
+    coarse_hbm, slots, correction_hbm,
     structure, medium, kmap, occupation, shift_a, shift_b,
     spread, factor, inner, square, panels, rows_tab, shift_tab,
-    row, own_rows, outgoing, first, part, total, block, slots,
-    load_sem, row_send, row_recv, first_send, first_recv, part_send, part_recv,
+    row, own_rows, outgoing, first, part, total, block, coarse, correction,
+    load_sem, out_sem, row_send, row_recv, first_send, first_recv, part_send, part_recv,
     total_send, total_recv, slot_send, slot_recv,
 ):
     pairs = (
@@ -667,7 +667,8 @@
                     out = jnp.where(line == at, lanes, out)
         block[e] = out
     slot_x.start(own_block)
-    slots[ka] = block[...]
+    own = pltpu.make_async_copy(block, slots.at[ka], out_sem.at[0])
+    own.start()
     moments = [
         moment_stage(
             rows[e][1][0], rows[e][2][0], tc_all[e][0], tb_all[e], tc_all[e][1], found[e][0],
@@ -685,9 +686,28 @@
                 coarse[e, c] = value
 
             coarse_out(found[e][0][c], tab, store)
+    leave = [
+        pltpu.make_async_copy(coarse, coarse_hbm, out_sem.at[1]),
+        pltpu.make_async_copy(correction, correction_hbm, out_sem.at[2]),
+    ]
+    for copy in leave:
+        copy.start()
     slot_x.wait(own_block)
-    for e in energies:
-        for at in range(n_ka):
+    rows_x.drain(own_row)
+    first_x.drain(own_sums)
+    part_x.drain(own_part)
+    total_x.drain(own_total)
+    slot_x.drain(own_block)
+    own.wait()
+    for copy in leave:
+        copy.wait()
+
+
+def output_kernel(coarse, slots, correction, coarse_to, average, correction_to):
+    coarse_to[...] = coarse[...]
+    correction_to[...] = correction[...]
+    for e in range(ENERGIES):
+        for at in range(slots.shape[0]):
             for c in range(2):
                 for site in range(2):
                     for side in range(2):
@@ -696,17 +716,6 @@
                         average[e, c, to : to + 1, side * LANES : side * LANES + LANES] = slots[
                             at, e, of : of + 1, :
                         ]
-    rows_x.drain(own_row)
-    first_x.drain(own_sums)
-    part_x.drain(own_part)
-    total_x.drain(own_total)
-    slot_x.drain(own_block)
-
-
-def output_kernel(coarse, average, correction, coarse_to, average_to, correction_to):
-    coarse_to[...] = coarse[...]
-    average_to[...] = average[...]
-    correction_to[...] = correction[...]
 
 
 def shape(*dims):
@@ -735,9 +744,9 @@
     )
     results = pl.pallas_call(
         functools.partial(kernel, per_moment, n_ka, n_cfg),
-        out_shape=shapes,
+        out_shape=(shapes[0], shape(n_ka, ENERGIES, 8, LANES), shapes[2]),
         in_specs=[any_spec] * 4 + [SMEM_SPEC] + [any_spec] * 2,
-        out_specs=(VMEM_SPEC,) * 3,
+        out_specs=(any_spec,) * 3,
         scratch_shapes=[
             vmem(*kdims), vmem(ENERGIES, 2, CHANS, CHANS, MOMS),
             pltpu.VMEM((1, LANES), jnp.int32), pltpu.VMEM((1, SITES), jnp.int32),
@@ -750,8 +759,9 @@
             vmem(n_cfg, ENERGIES, 8, LANES), vmem(n_cfg, ENERGIES, 8, LANES),
             vmem(n_ka, ENERGIES + 1, 8, LANES),
             vmem(n_cfg, ENERGIES, 8, LANES),
-            vmem(ENERGIES, 8, LANES), vmem(n_ka, ENERGIES, 8, LANES),
-            dma((6,)),
+            vmem(ENERGIES, 8, LANES),
+            vmem(ENERGIES, 2, CHANS, CHANS, MOMS), vmem(ENERGIES, 2, LANES),
+            dma((6,)), dma((3,)),
             dma((n_cfg,)), dma((n_cfg,)),
             dma((n_cfg,)), dma((n_cfg,)),
             dma((n_ka,)), dma((n_ka,)),

time: 35.3 us -> 34.9 us (0.989)
  Pallas kernels: 33.8 us -> 33.4 us
    pallas_call x1, Pallas kernels: 31.8 us -> 31.4 us  [per_device(): pl.pallas_call(functools.partial(kernel, per_moment, n_ka, n_cfg), out_sh...]
where the time goes in v8:
time: 34.9 us; the launch traced here: 34.7 us
  Pallas kernels  33.4 us (96%)
  between operations  1.29 us (4%)
    pallas_call x1, Pallas kernels, per_device(): pl.pallas_call(functools.partial(kernel, per_moment, n_ka, n_cfg), out_sh...  31.4 us
    pallas_call x1, Pallas kernels, per_device(): pl.pallas_call(output_kernel, out_shape=shapes, in_specs=[VMEM_SPEC] * 3,...  2.05 us

profile of v8, /device:TPU:1, one launch (start us, length us, event | category | flops | bytes accessed | tf_op | source)
XLA Modules:
  0.0 34.7 jit_solution(12594115893108014416)
XLA Ops:
  1.3 31.4 %shard_map.94 = (f32[2,2,16,16,16]{4,3,2,1,0:T(8,128)}, f32[16,2,8,128]{3,2,1,0:T(8,128)}, f32[2,2,128]{2,1,0:T(2,128)}) custom-call(f32[2,2,16,16,128]{4,3,2,1,0:T(8,128)} %structure_hbm.1, f32[2,2,16,16,16]{4,3,2,1,0:T(8,128)} %medium_hbm.1, s32[1,128]{1,0:T(1,128)} %bitcast.1, s32[1,16]{1,0:T(1,128)} %occupation_hbm.1, f32[1]{0:T(128)S(6)} %copy.10.weight, ...), custom_call_target="tpu_custom_call" | custom-call | tf_op jit(solution)/shard_map/pallas_call | solution.py:745
  32.7 2.0 %shard_map.95 = (f32[2,2,16,16,16]{4,3,2,1,0:T(8,128)}, f32[2,2,32,256]{3,2,1,0:T(8,128)}, f32[2,2,128]{2,1,0:T(2,128)}) custom-call(f32[2,2,16,16,16]{4,3,2,1,0:T(8,128)} %get-tuple-element.6.coarse, f32[16,2,8,128]{3,2,1,0:T(8,128)} %get-tuple-element.7.slots, f32[2,2,128]{2,1,0:T(2,128)} %get-tuple-element.8.correction), custom_call_target="tpu_custom_call" | custom-call | tf_op jit(solution)/shard_map/pallas_call | solution.py:775

commit v9 on v8

--- a/solution.py
+++ b/solution.py
@@ -267,21 +267,49 @@
     return b, c
 
 
-def coarse_panels(y, y_b, y_c, y_all, sum_t, tab, per_moment):
+def left_panel(y, sum_t, tab, per_moment):
     left = cdot(y, block_diag_c(sum_t, tab), NT)
-    scale = 1.0 / per_moment
-    left = (left[0] * scale, left[1] * scale)
+    return left[0] * (1.0 / per_moment), left[1] * (1.0 / per_moment)
+
+
+def site_matrix(parts, tab):
+    both = jnp.concatenate([parts[0][0], parts[0][1], parts[1][0], parts[1][1]], axis=0)
+
+    def fold(full):
+        return full[:WIDE] + full[WIDE : 2 * WIDE], full[2 * WIDE : 3 * WIDE] + full[3 * WIDE :]
+
+    re_cos, im_cos = fold(dot(both, tab.wave_cos, NT))
+    re_sin, im_sin = fold(dot(both, tab.wave_sin, NT))
+    scale = 1.0 / SITES
+    return csplit(((re_cos + im_sin) * scale, (im_cos - re_sin) * scale))
+
+
+def site_phases(site0):
+    mom = iota((16, WIDE), 1) >> 4
+    return cos_sin(quarter_turns(mom, site0 + (iota((16, WIDE), 0) >> 3)))
+
+
+def more_rows(known, left, line, phases, matrices):
+    cos, sin = phases
+    lr, li = jnp.broadcast_to(line[0], (16, WIDE)), jnp.broadcast_to(line[1], (16, WIDE))
+    both = (
+        jnp.concatenate([left[0], lr * cos - li * sin], axis=0),
+        jnp.concatenate([left[1], lr * sin + li * cos], axis=0),
+    )
     out = []
-    for base, parts in zip((y, y_b, y_c), y_all):
-        step = cdot(left, parts)
-        out.append((base[0] + step[0], base[1] + step[1]))
+    for (top, own), matrix in zip(known, matrices):
+        step = cdot(both, matrix)
+        out.append(
+            (
+                (top[0] + step[0][:16], top[1] + step[1][:16]),
+                (own[0] + step[0][16:], own[1] + step[1][16:]),
+            )
+        )
     return out
 
 
-def first_rows(panels, lines, tab, site0):
-    mom = iota((16, WIDE), 1) >> 4
-    second = (iota((16, WIDE), 0) >> 3).astype(jnp.int32)
-    cos, sin = cos_sin(quarter_turns(mom, site0 + second))
+def first_rows(panels, lines, tab, phases):
+    cos, sin = phases
     left_r, left_i = [], []
     for panel, line in zip(panels, lines):
         lr, li = jnp.broadcast_to(line[0], (16, WIDE)), jnp.broadcast_to(line[1], (16, WIDE))
@@ -621,6 +649,18 @@
         for e in energies
     ]
     kpoint_squares(spread, factor, inner, square, 1)
+    phases = site_phases(cfg * 2)
+    known = []
+    for e in energies:
+        lines = []
+        for at, panel in enumerate((y[e], y_b[e], y_c[e])):
+            panels[e, at, 0] = panel[0]
+            panels[e, at, 1] = panel[1]
+            lines.append(
+                (panels[e, at, 0, pl.ds(ka, 1), :], panels[e, at, 1, pl.ds(ka, 1), :])
+            )
+        known.append(first_rows((y[e], y_b[e], y_c[e]), lines, tab, phases))
+    matrices = [[site_matrix(parts, tab) for parts in y_all[0]]]
     part_x.wait(own_part)
     for e in energies:
         value = part[0, e]
@@ -630,22 +670,19 @@
     total_x.start(own_total)
     configs = jnp.concatenate([part[at, ENERGIES] for at in range(n_ka)], axis=0)
     moment_tables(configs, tab, rows_tab, shift_tab)
+    matrices.append([site_matrix(parts, tab) for parts in y_all[1]])
     total_x.wait(own_total)
-    found = []
+    lefts = []
     for e in energies:
         tiles = [total[at, e] for at in range(n_cfg)]
         sum_t = (gathered_panel(tiles, 0), gathered_panel(tiles, 4))
-        found.append(coarse_panels(y[e], y_b[e], y_c[e], y_all[e], sum_t, tab, per_moment))
+        lefts.append(left_panel(y[e], sum_t, tab, per_moment))
     rows = []
     for e in energies:
-        lines = []
-        for at, panel in enumerate(found[e]):
-            panels[e, at, 0] = panel[0]
-            panels[e, at, 1] = panel[1]
-            lines.append(
-                (panels[e, at, 0, pl.ds(ka, 1), :], panels[e, at, 1, pl.ds(ka, 1), :])
-            )
-        rows.append(first_rows(found[e], lines, tab, cfg * 2))
+        panels[e, 0, 0] = lefts[e][0]
+        panels[e, 0, 1] = lefts[e][1]
+        line_e = (panels[e, 0, 0, pl.ds(ka, 1), :], panels[e, 0, 1, pl.ds(ka, 1), :])
+        rows.append(more_rows(known[e], lefts[e], line_e, phases, matrices[e]))
     t_all = [translated_c(rows[e][0][0])[1] for e in energies]
     tb_all = [translated_c(rows[e][1][0])[1] for e in energies]
     tc_all = [translated_c(rows[e][2][0]) for e in energies]
@@ -669,10 +706,14 @@
     slot_x.start(own_block)
     own = pltpu.make_async_copy(block, slots.at[ka], out_sem.at[0])
     own.start()
+    found = []
+    for e in energies:
+        step = cdot(lefts[e], y_all[e][0])
+        found.append((y[e][0] + step[0], y[e][1] + step[1]))
     moments = [
         moment_stage(
-            rows[e][1][0], rows[e][2][0], tc_all[e][0], tb_all[e], tc_all[e][1], found[e][0],
-            block_diag_c(found[e][0], tab), wide[e][0], wide[e][1], shift_tab, tab,
+            rows[e][1][0], rows[e][2][0], tc_all[e][0], tb_all[e], tc_all[e][1], found[e],
+            block_diag_c(found[e], tab), wide[e][0], wide[e][1], shift_tab, tab,
         )
         for e in energies
     ]
@@ -685,7 +726,7 @@
             def store(value, e=e, c=c):
                 coarse[e, c] = value
 
-            coarse_out(found[e][0][c], tab, store)
+            coarse_out(found[e][c], tab, store)
     leave = [
         pltpu.make_async_copy(coarse, coarse_hbm, out_sem.at[1]),
         pltpu.make_async_copy(correction, correction_hbm, out_sem.at[2]),

time: 34.9 us -> 34.1 us (0.977)
  Pallas kernels: 33.4 us -> 32.7 us
    pallas_call x1, Pallas kernels: 31.4 us -> 30.6 us  [per_device(): pl.pallas_call(functools.partial(kernel, per_moment, n_ka, n_cfg), out_sh...]
where the time goes in v9:
time: 34.1 us; the launch traced here: 33.9 us
  Pallas kernels  32.7 us (96%)
  between operations  1.29 us (4%)
    pallas_call x1, Pallas kernels, per_device(): pl.pallas_call(functools.partial(kernel, per_moment, n_ka, n_cfg), out_sh...  30.6 us
    pallas_call x1, Pallas kernels, per_device(): pl.pallas_call(output_kernel, out_shape=shapes, in_specs=[VMEM_SPEC] * 3,...  2.05 us

profile of v9, /device:TPU:1, one launch (start us, length us, event | category | flops | bytes accessed | tf_op | source)
XLA Modules:
  0.0 33.9 jit_solution(13198906612502347084)
XLA Ops:
  1.3 30.6 %shard_map.94 = (f32[2,2,16,16,16]{4,3,2,1,0:T(8,128)}, f32[16,2,8,128]{3,2,1,0:T(8,128)}, f32[2,2,128]{2,1,0:T(2,128)}) custom-call(f32[2,2,16,16,128]{4,3,2,1,0:T(8,128)} %structure_hbm.1, f32[2,2,16,16,16]{4,3,2,1,0:T(8,128)} %medium_hbm.1, s32[1,128]{1,0:T(1,128)} %bitcast.1, s32[1,16]{1,0:T(1,128)} %occupation_hbm.1, f32[1]{0:T(128)S(6)} %copy.10.weight, ...), custom_call_target="tpu_custom_call" | custom-call | tf_op jit(solution)/shard_map/pallas_call | solution.py:786
  31.9 2.0 %shard_map.95 = (f32[2,2,16,16,16]{4,3,2,1,0:T(8,128)}, f32[2,2,32,256]{3,2,1,0:T(8,128)}, f32[2,2,128]{2,1,0:T(2,128)}) custom-call(f32[2,2,16,16,16]{4,3,2,1,0:T(8,128)} %get-tuple-element.6.coarse, f32[16,2,8,128]{3,2,1,0:T(8,128)} %get-tuple-element.7.slots, f32[2,2,128]{2,1,0:T(2,128)} %get-tuple-element.8.correction), custom_call_target="tpu_custom_call" | custom-call | tf_op jit(solution)/shard_map/pallas_call | solution.py:816

commit v10 on v9

--- a/solution.py
+++ b/solution.py
@@ -183,8 +183,8 @@
                 )
 
 
-def kpoint_squares(spread, factor, tau, square, e):
-    y, f, t, s = spread.at[e], factor.at[e], tau.at[e], square.at[e]
+def kpoint_tau(spread, factor, tau, work, e):
+    y, f, t, s = spread.at[e], factor.at[e], tau.at[e], work.at[e]
 
     def put_q(a, re, im):
         s[0, a] = f[0, a] + re
@@ -194,13 +194,18 @@
         t[0, a] = y[0, a] + re
         t[1, a] = y[1, a] + im
 
-    def put_s(a, re, im):
+    kpoint_mul(put_q, f, f)
+    kpoint_mul(put_t, s, y)
+
+
+def kpoint_square(tau, square, e):
+    t, s = tau.at[e], square.at[e]
+
+    def put(a, re, im):
         s[0, a] = re
         s[1, a] = im
 
-    kpoint_mul(put_q, f, f)
-    kpoint_mul(put_t, s, y)
-    kpoint_mul(put_s, t, t)
+    kpoint_mul(put, t, t)
 
 
 def config_row(occupation, weight, row):
@@ -625,7 +630,11 @@
     first[cfg] = outgoing[cfg]
     rows_x.start(own_row)
     own_rows[cfg] = row[...]
-    kpoint_squares(spread, factor, inner, square, 0)
+    kpoint_tau(spread, factor, inner, square, 0)
+    kpoint_square(inner, square, 0)
+    tab = Tables()
+    y = [medium_panels(medium, tab, e) for e in energies]
+    wide = [shift_panels(shift_a, shift_b, tab, e) for e in energies]
     rows_x.wait(own_row)
     line = iota((8, LANES), 0)
     group = jnp.zeros((8, LANES), F32)
@@ -639,16 +648,13 @@
         part[ka, e] = value
     part[ka, ENERGIES] = group
     part_x.start(own_part)
-    tab = Tables()
-    y = [medium_panels(medium, tab, e) for e in energies]
-    wide = [shift_panels(shift_a, shift_b, tab, e) for e in energies]
     y_b = [cdot(y[e], block_diag_c(wide[e][0], tab)) for e in energies]
     y_c = [cdot(y[e], block_diag_c(wide[e][1], tab)) for e in energies]
     y_all = [
         (block_diag_c(y[e], tab), block_diag_c(y_b[e], tab), block_diag_c(y_c[e], tab))
         for e in energies
     ]
-    kpoint_squares(spread, factor, inner, square, 1)
+    kpoint_tau(spread, factor, inner, square, 1)
     phases = site_phases(cfg * 2)
     known = []
     for e in energies:
@@ -671,6 +677,7 @@
     configs = jnp.concatenate([part[at, ENERGIES] for at in range(n_ka)], axis=0)
     moment_tables(configs, tab, rows_tab, shift_tab)
     matrices.append([site_matrix(parts, tab) for parts in y_all[1]])
+    kpoint_square(inner, square, 1)
     total_x.wait(own_total)
     lefts = []
     for e in energies:

time: 34.1 us -> 34.5 us (1.012)
    pallas_call x1, Pallas kernels: 30.6 us -> 31 us  [per_device(): pl.pallas_call(functools.partial(kernel, per_moment, n_ka, n_cfg), out_sh...]
where the time goes in v10:
time: 34.5 us; the launch traced here: 34.3 us
  Pallas kernels  33 us (96%)
  between operations  1.29 us (4%)
    pallas_call x1, Pallas kernels, per_device(): pl.pallas_call(functools.partial(kernel, per_moment, n_ka, n_cfg), out_sh...  31 us
    pallas_call x1, Pallas kernels, per_device(): pl.pallas_call(output_kernel, out_shape=shapes, in_specs=[VMEM_SPEC] * 3,...  2.05 us

profile of v10, /device:TPU:1, one launch (start us, length us, event | category | flops | bytes accessed | tf_op | source)
XLA Modules:
  0.0 34.3 jit_solution(7795980633449783736)
XLA Ops:
  1.3 31.0 %shard_map.94 = (f32[2,2,16,16,16]{4,3,2,1,0:T(8,128)}, f32[16,2,8,128]{3,2,1,0:T(8,128)}, f32[2,2,128]{2,1,0:T(2,128)}) custom-call(f32[2,2,16,16,128]{4,3,2,1,0:T(8,128)} %structure_hbm.1, f32[2,2,16,16,16]{4,3,2,1,0:T(8,128)} %medium_hbm.1, s32[1,128]{1,0:T(1,128)} %bitcast.1, s32[1,16]{1,0:T(1,128)} %occupation_hbm.1, f32[1]{0:T(128)S(6)} %copy.10.weight, ...), custom_call_target="tpu_custom_call" | custom-call | tf_op jit(solution)/shard_map/pallas_call | solution.py:793
  32.3 2.0 %shard_map.95 = (f32[2,2,16,16,16]{4,3,2,1,0:T(8,128)}, f32[2,2,32,256]{3,2,1,0:T(8,128)}, f32[2,2,128]{2,1,0:T(2,128)}) custom-call(f32[2,2,16,16,16]{4,3,2,1,0:T(8,128)} %get-tuple-element.6.coarse, f32[16,2,8,128]{3,2,1,0:T(8,128)} %get-tuple-element.7.slots, f32[2,2,128]{2,1,0:T(2,128)} %get-tuple-element.8.correction), custom_call_target="tpu_custom_call" | custom-call | tf_op jit(solution)/shard_map/pallas_call | solution.py:823

commit v11 on v10

--- a/solution.py
+++ b/solution.py
@@ -751,9 +751,23 @@
         copy.wait()
 
 
-def output_kernel(coarse, slots, correction, coarse_to, average, correction_to):
-    coarse_to[...] = coarse[...]
-    correction_to[...] = correction[...]
+def output_kernel(
+    coarse_from, slots_from, correction_from, coarse_to, average_to, correction_to,
+    coarse, slots, correction, average, sem,
+):
+    loads = [
+        pltpu.make_async_copy(slots_from, slots, sem.at[0]),
+        pltpu.make_async_copy(coarse_from, coarse, sem.at[1]),
+        pltpu.make_async_copy(correction_from, correction, sem.at[2]),
+    ]
+    stores = [
+        pltpu.make_async_copy(average, average_to, sem.at[3]),
+        pltpu.make_async_copy(coarse, coarse_to, sem.at[4]),
+        pltpu.make_async_copy(correction, correction_to, sem.at[5]),
+    ]
+    for load in loads:
+        load.start()
+    loads[0].wait()
     for e in range(ENERGIES):
         for at in range(slots.shape[0]):
             for c in range(2):
@@ -764,6 +778,12 @@
                         average[e, c, to : to + 1, side * LANES : side * LANES + LANES] = slots[
                             at, e, of : of + 1, :
                         ]
+    stores[0].start()
+    for load, store in zip(loads[1:], stores[1:]):
+        load.wait()
+        store.start()
+    for store in stores:
+        store.wait()
 
 
 def shape(*dims):
@@ -823,8 +843,13 @@
     return pl.pallas_call(
         output_kernel,
         out_shape=shapes,
-        in_specs=[VMEM_SPEC] * 3,
-        out_specs=(VMEM_SPEC,) * 3,
+        in_specs=[any_spec] * 3,
+        out_specs=(any_spec,) * 3,
+        scratch_shapes=[
+            vmem(ENERGIES, 2, CHANS, CHANS, MOMS), vmem(n_ka, ENERGIES, 8, LANES),
+            vmem(ENERGIES, 2, LANES), vmem(ENERGIES, 2, 2 * CHANS, WIDE), dma((6,)),
+        ],
+        compiler_params=pltpu.CompilerParams(vmem_limit_bytes=56 * 1024 * 1024),
     )(*results)
 
 

time: 34.5 us -> 34.6 us (level)
  no operation moved by 1% of the time
where the time goes in v11:
time: 34.6 us; the launch traced here: 34.4 us
  Pallas kernels  33 us (95%)
  between operations  1.45 us (4%)
    pallas_call x1, Pallas kernels, per_device(): pl.pallas_call(functools.partial(kernel, per_moment, n_ka, n_cfg), out_sh...  31 us
    pallas_call x1, Pallas kernels, per_device(): pl.pallas_call(output_kernel, out_shape=shapes, in_specs=[any_spec] * 3,...  1.96 us

profile of v11, /device:TPU:1, one launch (start us, length us, event | category | flops | bytes accessed | tf_op | source)
XLA Modules:
  0.0 34.4 jit_solution(18051703439131496807)
XLA Ops:
  1.3 31.0 %shard_map.94 = (f32[2,2,16,16,16]{4,3,2,1,0:T(8,128)}, f32[16,2,8,128]{3,2,1,0:T(8,128)}, f32[2,2,128]{2,1,0:T(2,128)}) custom-call(f32[2,2,16,16,128]{4,3,2,1,0:T(8,128)} %structure_hbm.1, f32[2,2,16,16,16]{4,3,2,1,0:T(8,128)} %medium_hbm.1, s32[1,128]{1,0:T(1,128)} %bitcast.1, s32[1,16]{1,0:T(1,128)} %occupation_hbm.1, f32[1]{0:T(128)S(6)} %copy.10.weight, ...), custom_call_target="tpu_custom_call" | custom-call | tf_op jit(solution)/shard_map/pallas_call | solution.py:813
  32.3 2.0 %shard_map.95 = (f32[2,2,16,16,16]{4,3,2,1,0:T(8,128)}, f32[2,2,32,256]{3,2,1,0:T(8,128)}, f32[2,2,128]{2,1,0:T(2,128)}) custom-call(f32[2,2,16,16,16]{4,3,2,1,0:T(8,128)} %get-tuple-element.6.coarse_from, f32[16,2,8,128]{3,2,1,0:T(8,128)} %get-tuple-element.7.slots_from, f32[2,2,128]{2,1,0:T(2,128)} %get-tuple-element.8.correction_from), custom_call_target="tpu_custom_call" | custom-call | tf_op jit(solution)/shard_map/pallas_call | solution.py:843
